TPU v7x, 512 devices: a whole 4x8x8 slice. The times are simulated.
512 devices in a mesh: grp: 16 (over y, core), mdl: 32 (over x, z).
Axes of the slice: x: 4, y: 8, z: 8, core: 2. Of those that a mesh axis runs over, the one named last changes fastest.
Arguments:
- row_states: bfloat16 [6144, 1024], P('grp', 'mdl'), may hold values from -6 to 6
- ffn_gain: bfloat16 [1024], replicated, may hold values from 0.25 to 1.75
- ffn_in: bfloat16 [1024, 32768], P('grp', 'mdl'), may hold values from -0.1875 to 0.1875
- ffn_out: bfloat16 [32768, 1024], P('mdl', 'grp'), may hold values from -0.0625 to 0.0625
- final_gain: bfloat16 [1024], replicated, may hold values from 0.25 to 1.75
- kv_weight: bfloat16 [2, 1024, 16384], P(None, None, 'mdl'), may hold values from -0.1875 to 0.1875
- queries: bfloat16 [4096, 16384], P('grp', 'mdl'), may hold values from -36 to 36
- attn_out: bfloat16 [16384, 1024], P('mdl'), may hold values from -0.75 to 0.75
- row_question: int32 [6144], replicated, may hold values from 0 to 15, as said below
Outputs:
- cross_out: bfloat16 [4096, 1024], P(('grp', 'mdl'))
Inputs may be any that keep to these rules, and one draw needn't show every extreme that they name: `row_question`: within each block of 384 rows (one row group) the rows are sorted by question; in every block each question owns a multiple of 8 rows, at least 8 and at most 72, and one question, drawn from the seed, owns exactly 72 rows of every block.
All inputs are finite; a program needn't handle non-finite values.
Results may differ from a plain program's by a relative error of at most 0.029.
Values may be sent and summed in bfloat16 or wider, within the bound.
No kernel may reach another device: no remote copies, remote signals or barrier semaphores. Data moves between devices by JAX's collectives and lax.ppermute only.
A program may use at most 64 MiB of HBM per device.

v0:
```python
import jax
import jax.numpy as jnp
from jax import lax
from jax.sharding import PartitionSpec as P

HEAD_DIM = 128


def rms_normalize(states, gain):
    wide = states.astype(jnp.float32)
    factor = lax.rsqrt(jnp.mean(wide * wide, axis=-1, keepdims=True) + 1e-06)
    return (wide * factor * gain.astype(jnp.float32)).astype(jnp.bfloat16)


def bucket_plan(row_question, rows_local, groups, my_group):
    capacity = 3 * rows_local // groups
    owners = row_question.reshape(groups, rows_local)
    owner_table = (owners[:, :, None] == jnp.arange(groups, dtype=jnp.int32)[None, None, :]).astype(
        jnp.int32
    )
    counts = jnp.sum(owner_table, axis=1)
    starts = jnp.cumsum(counts, axis=1) - counts
    slot_index = jnp.arange(capacity, dtype=jnp.int32)
    sent_counts = lax.dynamic_index_in_dim(counts, my_group, 0, keepdims=False)
    sent_starts = lax.dynamic_index_in_dim(starts, my_group, 0, keepdims=False)
    send_valid = slot_index[None, :] < sent_counts[:, None]
    send_rows = jnp.minimum(sent_starts[:, None] + slot_index[None, :], rows_local - 1)
    got_counts = lax.dynamic_index_in_dim(counts, my_group, 1, keepdims=False)
    got_valid = (slot_index[None, :] < got_counts[:, None]).reshape(-1)
    return (capacity, send_rows, send_valid, got_valid)


def pack_slots(source, send_rows, send_valid):
    picked = jnp.take(source, send_rows.reshape(-1), axis=0)
    picked = picked.reshape(send_rows.shape[0], send_rows.shape[1], source.shape[1])
    picked = jnp.where(send_valid[:, :, None], picked, jnp.zeros((), source.dtype))
    return picked.reshape(send_rows.shape[0], -1)


def local(
    row_states, ffn_gain, ffn_in, ffn_out, final_gain, kv_weight, queries, attn_out, row_question
):
    groups = lax.axis_size("grp")
    my_group = lax.axis_index("grp")
    rows_local = row_states.shape[0]
    full_rows = lax.all_gather(row_states, "mdl", axis=1, tiled=True)
    normed = rms_normalize(full_rows, ffn_gain)
    pre_active = jnp.dot(
        normed,
        lax.all_gather(ffn_in, "grp", axis=0, tiled=True),
        preferred_element_type=jnp.float32,
    )
    hidden = jnp.maximum(pre_active, 0.0).astype(jnp.bfloat16)
    ffn_terms = jnp.dot(
        hidden,
        lax.all_gather(ffn_out, "grp", axis=1, tiled=True),
        preferred_element_type=jnp.float32,
    )
    ffn_sum = lax.psum_scatter(ffn_terms, "mdl", scatter_dimension=1, tiled=True)
    enc_state = (row_states.astype(jnp.float32) + ffn_sum).astype(jnp.bfloat16)
    capacity, send_rows, send_valid, got_valid = bucket_plan(
        row_question, rows_local, groups, my_group
    )
    head_cols = kv_weight.shape[2]
    outgoing = pack_slots(enc_state, send_rows, send_valid)
    arrived = lax.all_to_all(outgoing, "grp", split_axis=0, concat_axis=0, tiled=True)
    slot_rows = lax.all_gather(arrived.reshape(groups * capacity, -1), "mdl", axis=1, tiled=True)
    encoded = rms_normalize(slot_rows, final_gain)
    projected = jnp.einsum(
        "rd,kdc->krc", encoded, kv_weight, preferred_element_type=jnp.float32
    ).astype(jnp.bfloat16)
    key_rows = projected[0]
    value_rows = projected[1]
    targets = queries.shape[0]
    heads_local = head_cols // HEAD_DIM
    query_heads = queries.reshape(targets, heads_local, HEAD_DIM)
    key_heads = key_rows.reshape(-1, heads_local, HEAD_DIM)
    value_heads = value_rows.reshape(-1, heads_local, HEAD_DIM)
    scores = jnp.einsum("thd,rhd->htr", query_heads, key_heads, preferred_element_type=jnp.float32)
    slot_mask = got_valid[None, None, :]
    scores = jnp.where(slot_mask, scores, -1e30)
    top_score = jnp.max(scores, axis=-1, keepdims=True)
    raised = jnp.where(slot_mask, jnp.exp(scores - top_score), 0.0)
    probabilities = (raised / jnp.sum(raised, axis=-1, keepdims=True)).astype(jnp.bfloat16)
    attended = jnp.einsum(
        "htr,rhd->thd", probabilities, value_heads, preferred_element_type=jnp.float32
    )
    attended = attended.astype(jnp.bfloat16).reshape(targets, head_cols)
    return lax.psum_scatter(
        jnp.dot(attended, attn_out, preferred_element_type=jnp.float32).astype(jnp.bfloat16),
        "mdl",
        scatter_dimension=0,
        tiled=True,
    )


def solution(mesh):
    in_specs = (
        P("grp", "mdl"),
        P(),
        P("grp", "mdl"),
        P("mdl", "grp"),
        P(),
        P(None, None, "mdl"),
        P("grp", "mdl"),
        P("mdl", None),
        P(),
    )
    out_specs = P(("grp", "mdl"), None)
    return jax.shard_map(local, mesh=mesh, in_specs=in_specs, out_specs=out_specs, check_vma=False)
```

profile of v0, /device:TPU:8, one launch (start us, length us, event | category | flops | bytes accessed | tf_op | source)
XLA Modules:
  0.0 669.9 jit_solution(2616351746955564816)
XLA Ops:
  6.5 0.0 copy-start
  6.5 0.0 all-gather.4.cloned.1.call-start
  6.5 0.7 all-gather.4.cloned.1.call-update
  7.3 0.0 all-gather.6.cloned.1.call-start
  7.3 0.7 all-gather.6.cloned.1.call-update
  8.0 0.0 reduce-scatter.3.cloned.1.call-start
  8.1 0.7 convert_element_type.51
  8.7 56.0 %all_gather.12 = bf16[384,1024]{0,1:T(8,128)(2,1)S(1)} all-gather(bf16[384,32]{0,1:T(8,128)(2,1)} %param.9), channel_id=1, replica_groups=mesh['grp'=16,'mdl'=32] {'mdl'}, dimensions={1}, use_global_device_ids=true | all-gather | bytes 811008 | tf_op jit(solution)/shard_map/all_gather | solution.py:46
  64.7 0.2 fusion.14
  64.9 0.0 copy-start.4
  64.9 0.0 all-gather.4.cloned.1.call-done
  65.0 33.6 %all-gather.6.cloned.1.call-done = bf16[1024,1024]{0,1:T(8,128)(2,1)} async-done(((bf16[1024,64]{0,1:T(8,128)(2,1)}), bf16[1024,1024]{0,1:T(8,128)(2,1)}) %all-gather.6.cloned.1.call-update) | async-done | bytes 2097168 | tf_op jit(solution)/shard_map/all_gather | solution.py:56
  98.5 5.6 fusion.22
  104.1 0.0 copy-start.3
  104.1 0.0 reduce-scatter.3.cloned.1.call-update
  104.1 0.0 all-gather.8.cloned.1.call-start
  104.2 0.0 copy-done.4
  104.2 0.4 convert_reduce_fusion
  104.6 0.2 reduce_window_sum.11
  104.8 0.1 add_minimum_fusion
  104.8 0.1 min.22
  104.9 0.1 iota_compare_fusion.2
  105.0 0.2 broadcast_in_dim.60
  105.2 0.2 broadcast_in_dim.61
  105.5 0.2 broadcast_in_dim.62
  105.7 0.2 broadcast_in_dim.63
  106.0 222.1 %reduce-scatter.3.cloned.1.call-done = f32[384,32]{0,1:T(8,128)} async-done(((f32[384,1024]{0,1:T(8,128)}), f32[384,32]{0,1:T(8,128)}) %reduce-scatter.3.cloned.1.call-update) | async-done | bytes 49168 | tf_op jit(solution)/shard_map/reduce_scatter | solution.py:59
  328.1 0.0 copy-done.3
  328.1 0.8 add_convert_fusion
  328.9 0.1 copy.28
  329.0 0.0 copy-start.5
  329.0 2.9 gather_fusion
  332.0 0.2 gather.7
  332.2 0.5 broadcast.116
  332.7 0.7 reduce.5
  333.4 13.6 %all_to_all.6 = bf16[16,2,1152]{2,1,0:T(2,128)(2,1)S(1)} all-to-all(bf16[16,2,1152]{2,1,0:T(2,128)(2,1)S(1)} %reshape.169), channel_id=1, replica_groups=mesh['grp'=16,'mdl'=32] {'grp'}, dimensions={0} | all-to-all | bytes 147456 | tf_op jit(solution)/shard_map/all_to_all | solution.py:66
  347.0 0.1 reshape.170
  347.0 0.4 reduce.1
  347.5 0.2 reshape.154
  347.7 0.8 copy.30
  348.5 0.0 all-gather.8.cloned.1.call-update
  348.5 0.0 reduce-scatter.5.cloned.1.call-start
  348.5 0.0 copy-done.5
  348.6 0.2 dynamic-slice_reduce_fusion
  348.7 0.1 iota_compare_fusion.1
  348.8 0.1 lt.86
  348.9 78.2 %all-gather.8.cloned.1.call-done = bf16[1152,1024]{0,1:T(8,128)(2,1)} async-done(((bf16[1152,32]{0,1:T(8,128)(2,1)}), bf16[1152,1024]{0,1:T(8,128)(2,1)}) %all-gather.8.cloned.1.call-update) | async-done | bytes 2359312 | tf_op jit(solution)/shard_map/all_gather | solution.py:67
  427.1 0.0 copy-start.1
  427.1 2.3 fusion.2
  429.4 0.0 copy-done
  429.4 0.0 copy-done.1
  429.5 3.5 fusion.8
  432.9 0.0 copy-start.6
  432.9 1.2 fusion.40
  434.2 0.0 copy-done.6
  434.2 5.5 fusion.41
  439.7 0.0 copy-start.2
  439.7 2.9 fusion.17
  442.6 0.0 copy-done.2
  442.6 1.3 convolution_convert_fusion.1
  443.9 0.0 reduce-scatter.5.cloned.1.call-update
  443.9 219.4 %reduce-scatter.5.cloned.1.call-done = bf16[8,1024]{1,0:T(8,128)(2,1)} async-done(((bf16[256,1024]{1,0:T(8,128)(2,1)}), bf16[8,1024]{1,0:T(8,128)(2,1)}) %reduce-scatter.5.cloned.1.call-update) | async-done | bytes 16400 | tf_op jit(solution)/shard_map/reduce_scatter | solution.py:89
  (9 shorter events, 0.1 us)
Async XLA Ops:
  6.5 422.9 %copy-start = (bf16[2,1024,512]{2,1,0:T(8,128)(2,1)S(1)}, bf16[2,1024,512]{2,1,0:T(8,128)(2,1)}, u32[]{:S(2)}) copy-start(bf16[2,1024,512]{2,1,0:T(8,128)(2,1)} %param.14) | copy-start | bytes 6291460
  6.5 58.4 %all-gather.4.cloned.1.call-start = ((), (), s32[]{:S(2)}) async-start(), calls=%async_computation.3 | async-start | bytes 2228224 | tf_op jit(solution)/shard_map/all_gather | solution.py:50
  7.3 91.3 %all-gather.6.cloned.1.call-start = ((), (), s32[]{:S(2)}) async-start(), calls=%async_computation.4 | async-start | bytes 2228224 | tf_op jit(solution)/shard_map/all_gather | solution.py:56
  8.0 320.1 %reduce-scatter.3.cloned.1.call-start = ((), (), s32[]{:S(2)}) async-start(), calls=%async_computation.5 | async-start | bytes 1622016 | tf_op jit(solution)/shard_map/reduce_scatter | solution.py:59
  64.9 39.3 %copy-start.4 = (s32[6144]{0:T(1024)S(1)}, s32[6144]{0:T(1024)}, u32[]{:S(2)}) copy-start(s32[6144]{0:T(1024)} %param.17) | copy-start | bytes 73732
  104.1 224.0 %copy-start.3 = (bf16[384,32]{0,1:T(8,128)(2,1)S(1)}, bf16[384,32]{0,1:T(8,128)(2,1)}, u32[]{:S(2)}) copy-start(bf16[384,32]{0,1:T(8,128)(2,1)} %param.9) | copy-start | bytes 73732
  104.1 322.9 %all-gather.8.cloned.1.call-start = ((), (), s32[]{:S(2)}) async-start(), calls=%async_computation.6 | async-start | bytes 2433024 | tf_op jit(solution)/shard_map/all_gather | solution.py:67
  329.0 19.5 %copy-start.5 = (bf16[1024]{0:T(1024)(128)(2,1)S(1)}, bf16[1024]{0:T(1024)(128)(2,1)}, u32[]{:S(2)}) copy-start(bf16[1024]{0:T(1024)(128)(2,1)} %param.13) | copy-start | bytes 6148
  348.5 314.8 %reduce-scatter.5.cloned.1.call-start = ((), (), s32[]{:S(2)}) async-start(), calls=%async_computation.7 | async-start | bytes 540672 | tf_op jit(solution)/shard_map/reduce_scatter | solution.py:89
  427.1 2.4 copy-start.1
  432.9 1.2 copy-start.6
  439.7 3.0 copy-start.2
Sparse Core Ops, SparseCore 0:
  9.5 46.1 all-gather.3
  57.7 40.7 all-gather.5
  104.3 223.7 reduce-scatter.2
  348.6 78.4 all-gather.7
  444.0 219.2 reduce-scatter.4
where the time goes:
time: 670 us
  waiting for transfers between devices  555 us (83%)
  blocking collectives  69.5 us (10%)
  matrix products  18.7 us (3%)
  between operations  13.3 us (2%)
  local copies, waits for them, and re-layouts  7.41 us (1%)
    reduce_scatter x1, waiting for transfers between devices, local(): lax.psum_scatter(ffn_terms, 'mdl', scatter_dimension=1, tiled=True)  222 us
    reduce_scatter x1, waiting for transfers between devices, local(): lax.psum_scatter(jnp.dot(attended, attn_out, preferred_element_type=jnp.f...  219 us
    all_gather x1, waiting for transfers between devices, local(): lax.all_gather(arrived.reshape(groups * capacity, -1), 'mdl', axis=1, til...  78.2 us
    all_gather x1, blocking collectives, local(): full_rows = lax.all_gather(row_states, 'mdl', axis=1, tiled=True)  56 us
    all_gather x1, waiting for transfers between devices, local(): lax.all_gather(ffn_out, 'grp', axis=1, tiled=True)  33.6 us
    all_to_all x1, blocking collectives, local(): lax.all_to_all(outgoing, 'grp', split_axis=0, concat_axis=0, tiled=True)  13.6 us
  transfers between devices with their start and end apart: 5, of which 4 were waited for; matrix products, arithmetic and copies ran while one was open for 0% of the time, Pallas kernels for 0%

commit v1 on v0

v1 whole, which is shorter than its diff:
```python
import jax
import jax.numpy as jnp
from jax import lax
from jax.sharding import Mesh, PartitionSpec as P

HEAD_DIM = 128
GRP = ("y", "core")
MDL = ("x", "z")


def swap_cores(value):
    return lax.ppermute(value, "core", [(0, 1), (1, 0)])


def normalize_columns(states, gain):
    wide = states.astype(jnp.float32)
    factor = lax.rsqrt(jnp.mean(wide * wide, axis=0, keepdims=True) + 1e-06)
    return (wide * factor * gain.astype(jnp.float32)[:, None]).astype(jnp.bfloat16)


def slot_plan(row_question, rows_local, groups, my_group):
    capacity = 3 * rows_local // groups
    owners = row_question.reshape(groups, rows_local)
    questions = jnp.arange(groups, dtype=jnp.int32)
    counts = jnp.sum((owners[:, :, None] == questions).astype(jnp.int32), axis=1)
    slots = jnp.arange(capacity, dtype=jnp.int32)
    mine = lax.dynamic_index_in_dim(owners, my_group, 0, keepdims=False)
    sent_counts = lax.dynamic_index_in_dim(counts, my_group, 0, keepdims=False)
    sent_starts = jnp.sum((mine[None, :] < questions[:, None]).astype(jnp.int32), axis=1)
    source = jnp.where(
        slots[None, :] < sent_counts[:, None], sent_starts[:, None] + slots[None, :], -1
    )
    got_counts = lax.dynamic_index_in_dim(counts, my_group, 1, keepdims=False)
    got_valid = (slots[None, :] < got_counts[:, None]).reshape(-1)
    rows = jnp.arange(rows_local, dtype=jnp.int32)
    pick = (rows[:, None] == source.reshape(1, -1)).astype(jnp.bfloat16)
    return capacity, pick, got_valid


def local(
    row_states, ffn_gain, ffn_in, ffn_out, final_gain, kv_weight, queries, attn_out, row_question
):
    groups = lax.axis_size(GRP)
    models = lax.axis_size(MDL)
    my_group = lax.axis_index(GRP)
    my_core = lax.axis_index("core")
    rows_local, feats_local = row_states.shape
    hid_local = ffn_in.shape[1]
    width = feats_local * models

    own_rows = row_states.T
    in_half = lax.all_gather(ffn_in, "y", axis=0, tiled=True)
    in_other = swap_cores(in_half)
    out_half = lax.all_gather(ffn_out.T, "y", axis=0, tiled=True)
    out_other = swap_cores(out_half)
    full_rows = lax.all_gather(own_rows, MDL, axis=0, tiled=True)
    normed = normalize_columns(full_rows, ffn_gain)
    halves = normed.reshape(-1, 2, ffn_in.shape[0], rows_local)
    mine = lax.dynamic_index_in_dim(halves, my_core, 1, keepdims=False).reshape(-1, rows_local)
    theirs = lax.dynamic_index_in_dim(halves, 1 - my_core, 1, keepdims=False)
    theirs = theirs.reshape(-1, rows_local)

    def contract(weight, columns):
        return lax.dot_general(
            weight, columns, (((0,), (0,)), ((), ())), preferred_element_type=jnp.float32
        )

    pre_active = contract(in_half, mine) + contract(in_other, theirs)
    hidden = jnp.maximum(pre_active, 0.0).astype(jnp.bfloat16)
    share_mine = jnp.dot(out_half, hidden, preferred_element_type=jnp.float32)
    share_other = jnp.dot(out_other, hidden, preferred_element_type=jnp.float32)
    share_mine = share_mine.astype(jnp.bfloat16).reshape(-1, 1, ffn_out.shape[1], rows_local)
    share_other = share_other.astype(jnp.bfloat16).reshape(-1, 1, ffn_out.shape[1], rows_local)
    first = my_core == 0
    shares = jnp.concatenate(
        [
            jnp.where(first, share_mine, share_other),
            jnp.where(first, share_other, share_mine),
        ],
        axis=1,
    ).reshape(models, feats_local, rows_local)
    arrived = lax.all_to_all(shares, MDL, 0, 0, tiled=True)
    ffn_sum = jnp.sum(arrived.astype(jnp.float32), axis=0)
    enc_state = (own_rows.astype(jnp.float32) + ffn_sum).astype(jnp.bfloat16)

    capacity, pick, got_valid = slot_plan(row_question, rows_local, groups, my_group)
    packed = jnp.dot(enc_state, pick, preferred_element_type=jnp.float32).astype(jnp.bfloat16)
    packed = packed.reshape(feats_local, groups, capacity).transpose(1, 0, 2)
    regrouped = lax.all_to_all(packed, GRP, 0, 0, tiled=True)
    slots = regrouped.transpose(1, 0, 2).reshape(feats_local, groups * capacity)
    slot_rows = lax.all_gather(slots, MDL, axis=0, tiled=True)
    encoded = normalize_columns(slot_rows, final_gain)

    projected = lax.dot_general(
        kv_weight, encoded, (((1,), (0,)), ((), ())), preferred_element_type=jnp.float32
    ).astype(jnp.bfloat16)
    head_cols = kv_weight.shape[2]
    heads_local = head_cols // HEAD_DIM
    targets = queries.shape[0]
    key_heads = projected[0].reshape(heads_local, HEAD_DIM, -1)
    value_heads = projected[1].reshape(heads_local, HEAD_DIM, -1)
    query_heads = queries.reshape(targets, heads_local, HEAD_DIM)
    scores = jnp.einsum("thd,hdr->htr", query_heads, key_heads, preferred_element_type=jnp.float32)
    slot_mask = got_valid[None, None, :]
    scores = jnp.where(slot_mask, scores, -1e30)
    top_score = jnp.max(scores, axis=-1, keepdims=True)
    raised = jnp.where(slot_mask, jnp.exp(scores - top_score), 0.0)
    probabilities = (raised / jnp.sum(raised, axis=-1, keepdims=True)).astype(jnp.bfloat16)
    attended = jnp.einsum(
        "htr,hdr->thd", probabilities, value_heads, preferred_element_type=jnp.float32
    )
    attended = attended.astype(jnp.bfloat16).reshape(targets, head_cols)
    partial = jnp.dot(attended, attn_out, preferred_element_type=jnp.float32).astype(jnp.bfloat16)
    partial = partial.reshape(models, targets // models, width)
    shares_out = lax.all_to_all(partial, MDL, 0, 0, tiled=True)
    return jnp.sum(shares_out.astype(jnp.float32), axis=0).astype(jnp.bfloat16)


def solution(mesh):
    fine = Mesh(mesh.devices.reshape(-1, 2, 4, 8), ("y", "core", "x", "z"))
    in_specs = (
        P(GRP, MDL),
        P(),
        P(GRP, MDL),
        P(MDL, GRP),
        P(),
        P(None, None, MDL),
        P(GRP, MDL),
        P(MDL, None),
        P(),
    )
    out_specs = P(GRP + MDL, None)
    return jax.shard_map(local, mesh=fine, in_specs=in_specs, out_specs=out_specs, check_vma=False)
```

time: 670 us -> 276 us (0.41)
  the two profiles are of different devices: /device:TPU:8 before, /device:TPU:64 now
where the time goes in v1:
time: 276 us; the launch traced here: 275 us
  waiting for transfers between devices  130 us (47%)
  blocking collectives  88 us (32%)
  matrix products  17.7 us (6%)
  starting transfers between devices  14.4 us (5%)
  between operations  13.4 us (5%)
  other arithmetic  5.91 us (2%)
  local copies, waits for them, and re-layouts  5.66 us (2%)
    all_gather x1, waiting for transfers between devices, local(): slot_rows = lax.all_gather(slots, MDL, axis=0, tiled=True)  75.7 us
    all_gather x1, blocking collectives, local(): full_rows = lax.all_gather(own_rows, MDL, axis=0, tiled=True)  54.6 us
    all_gather x1, waiting for transfers between devices, local(): out_half = lax.all_gather(ffn_out.T, 'y', axis=0, tiled=True)  30.5 us
    all_to_all x1, waiting for transfers between devices, local(): arrived = lax.all_to_all(shares, MDL, 0, 0, tiled=True)  22.6 us
    all_to_all x1, blocking collectives, local(): shares_out = lax.all_to_all(partial, MDL, 0, 0, tiled=True)  20.4 us
    all_to_all x1, blocking collectives, local(): regrouped = lax.all_to_all(packed, GRP, 0, 0, tiled=True)  13 us
    all_to_all x1, starting transfers between devices, local(): arrived = lax.all_to_all(shares, MDL, 0, 0, tiled=True)  10.5 us
  transfers between devices with their start and end apart: 6, of which 3 were waited for; matrix products, arithmetic and copies ran while one was open for 3% of the time, Pallas kernels for 0%

profile of v1, /device:TPU:64, one launch (start us, length us, event | category | flops | bytes accessed | tf_op | source)
XLA Modules:
  0.0 275.3 jit_solution(3904572690339405534)
XLA Ops:
  6.5 0.0 copy-start
  6.5 0.0 all-gather.4.cloned.1.call-start
  6.5 0.7 all-gather.4.cloned.1.call-update
  7.3 0.0 all-gather.6.cloned.1.call-start
  7.3 0.7 all-gather.6.cloned.1.call-update
  8.0 0.7 convert_element_type.71
  8.7 54.6 %all_gather.12 = bf16[1024,384]{1,0:T(8,128)(2,1)S(1)} all-gather(bf16[32,384]{1,0:T(8,128)(2,1)} %bitcast.83), channel_id=1, replica_groups=mesh['y'=8,'core'=2,'x'=4,'z'=8] {'x','z'}, dimensions={0}, use_global_device_ids=true | all-gather | bytes 811008 | tf_op jit(solution)/shard_map/all_gather | solution.py:56
  63.3 0.0 all-gather.4.cloned.1.call-done
  63.3 1.9 collective-permute-start
  65.2 0.2 fusion.14
  65.5 30.5 %all-gather.6.cloned.1.call-done = bf16[512,1024]{1,0:T(8,128)(2,1)} async-done(((bf16[64,1024]{1,0:T(8,128)(2,1)}), bf16[512,1024]{1,0:T(8,128)(2,1)}) %all-gather.6.cloned.1.call-update) | async-done | bytes 1048592 | tf_op jit(solution)/shard_map/all_gather | solution.py:54
  96.0 1.9 collective-permute-start.1
  97.9 1.1 fusion.16
  99.0 0.0 copy-start.2
  99.0 1.3 constant_dynamic-slice_fusion.1
  100.3 0.2 copy-done.2
  100.5 0.6 fusion.37
  101.1 0.0 copy-start.7
  101.1 0.0 collective-permute-done
  101.1 1.9 maximum_convert_fusion
  103.0 0.0 copy-done.7
  103.0 0.6 convolution_convert_fusion.4
  103.7 0.0 collective-permute-done.1
  103.7 1.8 select_bitcast_fusion.1
  105.5 0.2 copy.47
  105.7 0.2 copy.48
  105.9 0.0 copy-start.5
  106.0 0.1 pad_maximum_fusion
  106.1 0.0 copy-start.4
  106.1 1.0 copy.49
  107.0 10.5 %all-to-all-start = ((bf16[32,32,384]{2,1,0:T(8,128)(2,1)}), bf16[32,32,384]{2,1,0:T(8,128)(2,1)S(1)}, u32[]{:S(2)}, u32[]{:S(2)}) async-start(bf16[32,32,384]{2,1,0:T(8,128)(2,1)} %bitcast.71), calls=%async_computation | async-start | bytes 1572864 | tf_op jit(solution)/shard_map/all_to_all | solution.py:82
  117.5 0.0 all-gather.8.cloned.1.call-start
  117.6 0.0 copy-done.5
  117.6 0.4 convert_reduce_fusion.1
  118.0 0.1 convert_reduce_fusion.2
  118.1 0.1 add_select_fusion
  118.2 0.1 select_n.87
  118.3 22.6 %all-to-all-done = bf16[32,32,384]{2,1,0:T(8,128)(2,1)S(1)} async-done(((bf16[32,32,384]{2,1,0:T(8,128)(2,1)}), bf16[32,32,384]{2,1,0:T(8,128)(2,1)S(1)}, u32[]{:S(2)}, u32[]{:S(2)}) %all-to-all-start) | async-done | bytes 786464 | tf_op jit(solution)/shard_map/all_to_all | solution.py:82
  140.8 0.1 convert_reduce_fusion
  141.0 0.0 copy-done.4
  141.0 0.4 convolution_convert_fusion.1
  141.4 0.2 reshape.150
  141.7 13.0 %all_to_all.15 = bf16[16,32,72]{2,1,0:T(8,128)(2,1)S(1)} all-to-all(bf16[16,32,72]{2,1,0:T(8,128)(2,1)S(1)} %bitcast.79), channel_id=1, replica_groups=mesh['y'=8,'core'=2,'x'=4,'z'=8] {'y','core'}, dimensions={0} | all-to-all | bytes 147456 | tf_op jit(solution)/shard_map/all_to_all | solution.py:89
  154.6 0.1 copy.51
  154.7 0.8 reshape.151
  155.5 0.0 all-gather.8.cloned.1.call-update
  155.5 0.0 copy-done.6
  155.5 0.2 dynamic-slice_reduce_fusion
  155.7 0.1 iota_compare_fusion.4
  155.8 0.1 lt.90
  155.9 75.7 %all-gather.8.cloned.1.call-done = bf16[1024,1152]{1,0:T(8,128)(2,1)} async-done(((bf16[32,1152]{1,0:T(8,128)(2,1)}), bf16[1024,1152]{1,0:T(8,128)(2,1)}) %all-gather.8.cloned.1.call-update) | async-done | bytes 2359312 | tf_op jit(solution)/shard_map/all_gather | solution.py:91
  231.6 2.3 fusion.2
  234.0 0.0 copy-done
  234.0 0.0 copy-done.1
  234.0 3.5 %fusion.8 = bf16[2,512,1152]{2,1,0:T(8,128)(2,1)S(1)} fusion(bf16[2,1024,512]{2,1,0:T(8,128)(2,1)S(1)} %copy-done, bf16[1024,1152]{1,0:T(8,128)(2,1)S(1)} %copy-done.1, f32[1024]{0:T(1024)S(1)} %convert_element_type.82, f32[1152]{0:T(1024)S(1)} %add_rsqrt_fusion), kind=kOutput, calls=%fused_computation.13 | convolution fusion | flops 2421817344 | bytes 6824448 | tf_op jit(solution)/shard_map/dot_general | solution.py:94
  237.5 0.0 copy-start.8
  237.5 1.2 fusion.33
  238.7 0.0 copy-done.8
  238.7 5.5 %fusion.34 = (f32[4,256]{1,0:T(4,128)S(1)}, f32[4,256,1152]{1,2,0:T(8,128)}) fusion(bf16[4,128,1152]{2,1,0:T(8,128)(2,1)} %bitcast.78, pred[1152]{0:T(1024)(128)(4,1)S(1)} %lt.90, bf16[256,512]{1,0:T(8,128)(2,1)S(1)} %copy-done.8), kind=kOutput, calls=%fused_computation.59 | convolution fusion | flops 306709632 | bytes 6165632 | tf_op jit(solution)/shard_map/sub | solution.py:107
  244.2 2.9 %fusion.18 = bf16[4,128,256]{2,1,0:T(8,128)(2,1)S(1)} fusion(bf16[4,128,1152]{2,1,0:T(8,128)(2,1)S(1)} %bitcast.77, f32[4,256,1152]{1,2,0:T(8,128)} %get-tuple-element.12, f32[4,256]{1,0:T(4,128)S(1)} %get-tuple-element.11), kind=kOutput, calls=%fused_computation.31 | convolution fusion | flops 304480256 | bytes 6164480 | tf_op jit(solution)/shard_map/htr,hdr->thd/dot_general | solution.py:109
  247.2 0.0 copy-done.3
  247.2 0.5 fusion.17
  247.6 20.4 %all_to_all.16 = bf16[32,8,1024]{2,1,0:T(8,128)(2,1)S(1)} all-to-all(bf16[32,8,1024]{2,1,0:T(8,128)(2,1)S(1)} %fusion.17), channel_id=1, replica_groups=mesh['y'=8,'core'=2,'x'=4,'z'=8] {'x','z'}, dimensions={0} | all-to-all | bytes 1048576 | tf_op jit(solution)/shard_map/all_to_all | solution.py:115
  268.0 0.7 reduce_sum.72
  (10 shorter events, 0.1 us)
Async XLA Ops:
  6.5 227.4 %copy-start = (bf16[2,1024,512]{2,1,0:T(8,128)(2,1)S(1)}, bf16[2,1024,512]{2,1,0:T(8,128)(2,1)}, u32[]{:S(2)}) copy-start(bf16[2,1024,512]{2,1,0:T(8,128)(2,1)} %param.14) | copy-start | bytes 6291460
  6.5 56.8 %all-gather.4.cloned.1.call-start = ((), (), s32[]{:S(2)}) async-start(), calls=%async_computation.3 | async-start | bytes 1179648 | tf_op jit(solution)/shard_map/all_gather | solution.py:52
  7.3 88.8 %all-gather.6.cloned.1.call-start = ((), (), s32[]{:S(2)}) async-start(), calls=%async_computation.4 | async-start | bytes 1179648 | tf_op jit(solution)/shard_map/all_gather | solution.py:54
  63.3 37.8 %collective-permute-start = (bf16[512,1024]{1,0:T(8,128)(2,1)}, bf16[512,1024]{1,0:T(8,128)(2,1)}, u32[]{:S(2)}, u32[]{:S(2)}) collective-permute-start(bf16[512,1024]{1,0:T(8,128)(2,1)} %all-gather.4.cloned.1.call-done), channel_id=1, source_target_pairs={{0,32},{32,0},{1,33},{33,1},{2,34},{34,2},{3,35},{35,3},{4,36},{36... | collective-permute-start | bytes 3145736 | tf_op jit(solution)/shard_map/ppermute | solution.py:12
  96.0 7.6 %collective-permute-start.1 = (bf16[512,1024]{1,0:T(8,128)(2,1)}, bf16[512,1024]{1,0:T(8,128)(2,1)}, u32[]{:S(2)}, u32[]{:S(2)}) collective-permute-start(bf16[512,1024]{1,0:T(8,128)(2,1)} %all-gather.6.cloned.1.call-done), channel_id=1, source_target_pairs={{0,32},{32,0},{1,33},{33,1},{2,34},{34,2},{3,35},{35,3},{4,36},{36... | collective-permute-start | bytes 3145736 | tf_op jit(solution)/shard_map/ppermute | solution.py:12
  99.0 1.5 copy-start.2
  101.1 1.9 copy-start.7
  105.9 11.6 %copy-start.5 = (s32[6144]{0:T(1024)S(1)}, s32[6144]{0:T(1024)}, u32[]{:S(2)}) copy-start(s32[6144]{0:T(1024)} %param.17) | copy-start | bytes 73732
  106.1 34.9 %copy-start.4 = (bf16[384,32]{0,1:T(8,128)(2,1)S(1)}, bf16[384,32]{0,1:T(8,128)(2,1)}, u32[]{:S(2)}) copy-start(bf16[384,32]{0,1:T(8,128)(2,1)} %param.9) | copy-start | bytes 73732
  107.0 48.5 %copy-start.6 = (bf16[1024]{0:T(1024)(128)(2,1)S(1)}, bf16[1024]{0:T(1024)(128)(2,1)}, u32[]{:S(2)}) copy-start(bf16[1024]{0:T(1024)(128)(2,1)} %param.13) | copy-start | bytes 6148
  107.0 33.8 %all-to-all-start = ((bf16[32,32,384]{2,1,0:T(8,128)(2,1)}), bf16[32,32,384]{2,1,0:T(8,128)(2,1)S(1)}, u32[]{:S(2)}, u32[]{:S(2)}) async-start(bf16[32,32,384]{2,1,0:T(8,128)(2,1)} %bitcast.71), calls=%async_computation | async-start | bytes 1572864 | tf_op jit(solution)/shard_map/all_to_all | solution.py:82
  117.5 114.1 %all-gather.8.cloned.1.call-start = ((), (), s32[]{:S(2)}) async-start(), calls=%async_computation.5 | async-start | bytes 2433024 | tf_op jit(solution)/shard_map/all_gather | solution.py:91
  231.6 2.4 copy-start.1
  237.5 1.2 copy-start.8
  244.2 3.0 %copy-start.3 = (bf16[512,1024]{1,0:T(8,128)(2,1)S(1)}, bf16[512,1024]{1,0:T(8,128)(2,1)}, u32[]{:S(2)}) copy-start(bf16[512,1024]{1,0:T(8,128)(2,1)} %param.16) | copy-start | bytes 3145732
Sparse Core Ops, SparseCore 0:
  9.4 44.6 all-gather.3
  56.2 39.7 all-gather.5
  155.6 75.9 all-gather.7

commit v2 on v1

--- a/solution.py
+++ b/solution.py
@@ -16,6 +16,16 @@
     wide = states.astype(jnp.float32)
     factor = lax.rsqrt(jnp.mean(wide * wide, axis=0, keepdims=True) + 1e-06)
     return (wide * factor * gain.astype(jnp.float32)[:, None]).astype(jnp.bfloat16)
+
+
+def spread(value, axes):
+    copies = jnp.broadcast_to(value[None], (lax.axis_size(axes),) + value.shape)
+    return lax.all_to_all(copies, axes, 0, 0, tiled=True).reshape(-1, value.shape[-1])
+
+
+def shift(value, step):
+    size = lax.axis_size("x")
+    return lax.ppermute(value, "x", [(i, (i + step) % size) for i in range(size)])
 
 
 def slot_plan(row_question, rows_local, groups, my_group):
@@ -49,11 +59,12 @@
     width = feats_local * models
 
     own_rows = row_states.T
-    in_half = lax.all_gather(ffn_in, "y", axis=0, tiled=True)
-    in_other = swap_cores(in_half)
-    out_half = lax.all_gather(ffn_out.T, "y", axis=0, tiled=True)
-    out_other = swap_cores(out_half)
-    full_rows = lax.all_gather(own_rows, MDL, axis=0, tiled=True)
+    both = jnp.concatenate([ffn_in, ffn_out.T], axis=1)
+    both_half = lax.all_gather(both, "y", axis=0, tiled=True)
+    both_other = swap_cores(both_half)
+    in_half, out_half = both_half[:, :hid_local], both_half[:, hid_local:]
+    in_other, out_other = both_other[:, :hid_local], both_other[:, hid_local:]
+    full_rows = spread(own_rows, MDL)
     normed = normalize_columns(full_rows, ffn_gain)
     halves = normed.reshape(-1, 2, ffn_in.shape[0], rows_local)
     mine = lax.dynamic_index_in_dim(halves, my_core, 1, keepdims=False).reshape(-1, rows_local)
@@ -88,11 +99,21 @@
     packed = packed.reshape(feats_local, groups, capacity).transpose(1, 0, 2)
     regrouped = lax.all_to_all(packed, GRP, 0, 0, tiled=True)
     slots = regrouped.transpose(1, 0, 2).reshape(feats_local, groups * capacity)
-    slot_rows = lax.all_gather(slots, MDL, axis=0, tiled=True)
-    encoded = normalize_columns(slot_rows, final_gain)
+    near = spread(slots, "z")
+    behind, ahead = shift(near, 1), shift(near, -1)
+    half = near.shape[0] // 2
+    far = jnp.concatenate([shift(behind[:half], 1), shift(ahead[half:], -1)], axis=0)
+    slot_rows = jnp.concatenate([near, behind, ahead, far], axis=0)
+    my_x = lax.axis_index("x")
+    ring = [(my_x + step) % lax.axis_size("x") for step in (0, 3, 1, 2)]
+    gains = final_gain.reshape(len(ring), -1)
+    turned_gain = jnp.concatenate([lax.dynamic_index_in_dim(gains, i, 0, False) for i in ring])
+    banks = kv_weight.reshape(2, len(ring), -1, kv_weight.shape[2])
+    turned = jnp.concatenate([lax.dynamic_index_in_dim(banks, i, 1, False) for i in ring], axis=1)
+    encoded = normalize_columns(slot_rows, turned_gain)
 
     projected = lax.dot_general(
-        kv_weight, encoded, (((1,), (0,)), ((), ())), preferred_element_type=jnp.float32
+        turned, encoded, (((1,), (0,)), ((), ())), preferred_element_type=jnp.float32
     ).astype(jnp.bfloat16)
     head_cols = kv_weight.shape[2]
     heads_local = head_cols // HEAD_DIM

time: 276 us -> 215 us (0.78)
  blocking collectives: 88 us -> 36 us
  waiting for transfers between devices: 130 us -> 83.6 us
  starting transfers between devices: 14.4 us -> 43.2 us
  local copies, waits for them, and re-layouts: 5.66 us -> 15.3 us
    all_gather x3 -> x1, waiting for transfers between devices: 106 us -> 34.2 us  [local(): both_half = lax.all_gather(both, 'y', axis=0, tiled=True)]
    all_gather x1 -> x0, blocking collectives: 54.6 us -> none  [local(): full_rows = lax.all_gather(own_rows, MDL, axis=0, tiled=True)]
    all_to_all x0 -> x2, waiting for transfers between devices: none -> 18.3 us  [spread(): lax.all_to_all(copies, axes, 0, 0, tiled=True).reshape(-1, value.shape[-1])]
    all_to_all x0 -> x2, starting transfers between devices: none -> 16.6 us  [spread(): lax.all_to_all(copies, axes, 0, 0, tiled=True).reshape(-1, value.shape[-1])]
    ppermute x0 -> x4, starting transfers between devices: none -> 14.3 us  [shift(): lax.ppermute(value, 'x', [(i, (i + step) % size) for i in range(size)])]
    unnamed x18 -> x24, local copies, waits for them, and re-layouts: 0.22 us -> 6.94 us
    ppermute x0 -> x4, waiting for transfers between devices: none -> 6.57 us  [shift(): lax.ppermute(value, 'x', [(i, (i + step) % size) for i in range(size)])]
    all_to_all x1, blocking collectives: 20.4 us -> 23.4 us  [local(): shares_out = lax.all_to_all(partial, MDL, 0, 0, tiled=True)]
  transfers between devices with their start and end apart: 6 -> 9, of which waited for: 3 -> 6; matrix products, arithmetic and copies ran while one was open for 3% -> 7% of each run, Pallas kernels for 0% -> 0%
where the time goes in v2:
time: 215 us; the launch traced here: 214 us
  waiting for transfers between devices  83.6 us (39%)
  starting transfers between devices  43.2 us (20%)
  blocking collectives  36 us (17%)
  matrix products  17.3 us (8%)
  local copies, waits for them, and re-layouts  15.3 us (7%)
  between operations  13.7 us (6%)
  other arithmetic  5.22 us (2%)
    all_gather x1, waiting for transfers between devices, local(): both_half = lax.all_gather(both, 'y', axis=0, tiled=True)  34.2 us
    all_to_all x1, blocking collectives, local(): shares_out = lax.all_to_all(partial, MDL, 0, 0, tiled=True)  23.4 us
    all_to_all x1, waiting for transfers between devices, local(): arrived = lax.all_to_all(shares, MDL, 0, 0, tiled=True)  22.5 us
    all_to_all x2, waiting for transfers between devices, spread(): lax.all_to_all(copies, axes, 0, 0, tiled=True).reshape(-1, value.shape[-1])  18.3 us
    all_to_all x2, starting transfers between devices, spread(): lax.all_to_all(copies, axes, 0, 0, tiled=True).reshape(-1, value.shape[-1])  16.6 us
    ppermute x4, starting transfers between devices, shift(): lax.ppermute(value, 'x', [(i, (i + step) % size) for i in range(size)])  14.3 us
    all_to_all x1, blocking collectives, local(): regrouped = lax.all_to_all(packed, GRP, 0, 0, tiled=True)  12.6 us
    all_to_all x1, starting transfers between devices, local(): arrived = lax.all_to_all(shares, MDL, 0, 0, tiled=True)  10.3 us
  transfers between devices with their start and end apart: 9, of which 6 were waited for; matrix products, arithmetic and copies ran while one was open for 7% of the time, Pallas kernels for 0%

profile of v2, /device:TPU:64, one launch (start us, length us, event | category | flops | bytes accessed | tf_op | source)
XLA Modules:
  0.0 214.4 jit_solution(8023139417028859776)
XLA Ops:
  6.5 0.0 copy-start
  6.5 1.8 pad_maximum_fusion.1
  8.4 0.0 all-gather.2.cloned.1.call-update
  8.4 1.7 broadcast_in_dim.26
  10.1 12.6 %all-to-all-start = ((bf16[32,32,384]{2,1,0:T(8,128)(2,1)}), bf16[32,32,384]{2,1,0:T(8,128)(2,1)S(1)}, u32[]{:S(2)}, u32[]{:S(2)}) async-start(bf16[32,32,384]{2,1,0:T(8,128)(2,1)} %broadcast_in_dim.26), calls=%async_computation | async-start | bytes 1572864 | tf_op jit(solution)/shard_map/all_to_all | solution.py:23
  22.7 34.2 %all-gather.2.cloned.1.call-done = bf16[512,2048]{1,0:T(8,128)(2,1)} async-done(((bf16[64,2048]{1,0:T(8,128)(2,1)}), bf16[512,2048]{1,0:T(8,128)(2,1)}) %all-gather.2.cloned.1.call-update) | async-done | bytes 2097168 | tf_op jit(solution)/shard_map/all_gather | solution.py:63
  56.9 1.9 collective-permute-start
  58.8 0.1 reshape.210
  58.9 0.0 all-to-all-done
  58.9 0.2 multiply_reduce_fusion
  59.1 0.2 multiply_convert_fusion
  59.4 0.1 constant_dynamic-slice_fusion.6
  59.5 1.0 copy-done.7
  60.5 0.8 fusion.24
  61.2 2.0 collective-permute-done
  63.3 2.0 maximum_convert_fusion
  65.2 0.7 convolution_convert_fusion.4
  66.0 1.9 broadcast_select_fusion.1
  67.9 0.0 copy-start.4
  67.9 0.0 copy-start.3
  67.9 1.0 pad_maximum_fusion
  68.9 10.3 %all-to-all-start.1 = ((bf16[32,32,384]{2,1,0:T(8,128)(2,1)}), bf16[32,32,384]{2,1,0:T(8,128)(2,1)S(1)}, u32[]{:S(2)}, u32[]{:S(2)}) async-start(bf16[32,32,384]{2,1,0:T(8,128)(2,1)} %bitcast.14), calls=%async_computation.1 | async-start | bytes 1572864 | tf_op jit(solution)/shard_map/all_to_all | solution.py:93
  79.3 0.4 convert_reduce_fusion.1
  79.7 0.1 convert_reduce_fusion.2
  79.8 0.1 add_select_fusion
  79.9 0.1 select_n.124
  80.0 22.5 %all-to-all-done.1 = bf16[32,32,384]{2,1,0:T(8,128)(2,1)S(1)} async-done(((bf16[32,32,384]{2,1,0:T(8,128)(2,1)}), bf16[32,32,384]{2,1,0:T(8,128)(2,1)S(1)}, u32[]{:S(2)}, u32[]{:S(2)}) %all-to-all-start.1) | async-done | bytes 786464 | tf_op jit(solution)/shard_map/all_to_all | solution.py:93
  102.5 0.1 convert_reduce_fusion
  102.6 0.4 convolution_convert_fusion.1
  103.1 0.2 reshape.203
  103.3 12.6 %all_to_all.25 = bf16[16,32,72]{2,1,0:T(8,128)(2,1)S(1)} all-to-all(bf16[16,32,72]{2,1,0:T(8,128)(2,1)S(1)} %bitcast.82), channel_id=1, replica_groups=mesh['y'=8,'core'=2,'x'=4,'z'=8] {'y','core'}, dimensions={0} | all-to-all | bytes 147456 | tf_op jit(solution)/shard_map/all_to_all | solution.py:100
  115.9 0.1 copy.65
  116.0 0.2 broadcast_in_dim.32
  116.2 0.9 broadcast_in_dim.56
  117.0 4.1 %all-to-all-start.3 = ((bf16[8,32,1152]{2,1,0:T(8,128)(2,1)}), bf16[8,32,1152]{2,1,0:T(8,128)(2,1)S(1)}, u32[]{:S(2)}, u32[]{:S(2)}) async-start(bf16[8,32,1152]{2,1,0:T(8,128)(2,1)} %broadcast_in_dim.56), calls=%async_computation.3 | async-start | bytes 1179648 | tf_op jit(solution)/shard_map/all_to_all | solution.py:23
  121.1 18.3 %all-to-all-done.3 = bf16[8,32,1152]{2,1,0:T(8,128)(2,1)S(1)} async-done(((bf16[8,32,1152]{2,1,0:T(8,128)(2,1)}), bf16[8,32,1152]{2,1,0:T(8,128)(2,1)S(1)}, u32[]{:S(2)}, u32[]{:S(2)}) %all-to-all-start.3) | async-done | bytes 589856 | tf_op jit(solution)/shard_map/all_to_all | solution.py:23
  139.4 2.5 %collective-permute-start.1 = (bf16[256,1152]{1,0:T(8,128)(2,1)S(1)}, bf16[256,1152]{1,0:T(8,128)(2,1)}, u32[]{:S(2)}, u32[]{:S(2)}) collective-permute-start(bf16[256,1152]{1,0:T(8,128)(2,1)S(1)} %bitcast.72), channel_id=1, source_target_pairs={{0,8},{8,16},{16,24},{24,0},{1,9},{9,17},{17,25},{25,1},{2,10},{10... | collective-permute-start | bytes 1769480 | tf_op jit(solution)/shard_map/ppermute | solution.py:28
  141.9 4.5 %collective-permute-start.2 = (bf16[256,1152]{1,0:T(8,128)(2,1)S(1)}, bf16[256,1152]{1,0:T(8,128)(2,1)}, u32[]{:S(2)}, u32[]{:S(2)}) collective-permute-start(bf16[256,1152]{1,0:T(8,128)(2,1)S(1)} %bitcast.73), channel_id=1, source_target_pairs={{0,24},{8,0},{16,8},{24,16},{1,25},{9,1},{17,9},{25,17},{2,26},{10... | collective-permute-start | bytes 1769480 | tf_op jit(solution)/shard_map/ppermute | solution.py:28
  146.4 2.5 %constant_dynamic-slice_fusion.11 = (bf16[2,1,256,512]{3,2,1,0:T(8,128)(2,1)S(1)}, bf16[2,1,256,512]{3,2,1,0:T(8,128)(2,1)S(1)}, bf16[2,1,256,512]{3,2,1,0:T(8,128)(2,1)S(1)}, bf16[2,1,256,512]{3,2,1,0:T(8,128)(2,1)}) fusion(bf16[2,4,256,512]{3,2,1,0:T(8,128)(2,1)} %bitcast.75, s32[]{:T(128)S(6)} %select_n.108, s32[]{:T(128)S(6)} %select_n.112, ...), kind=kLoop, calls=%fused_computation.75 | loop fusion | bytes 4194320 | tf_op jit(solution)/shard_map/jit(dynamic_index_in_dim)/dynamic_slice | solution.py:112
  149.0 2.1 copy.74
  151.0 1.0 copy.73
  152.0 0.2 copy.72
  152.2 0.2 copy.71
  152.4 0.2 dynamic-slice_reduce_fusion
  152.6 0.1 iota_compare_fusion.4
  152.7 0.1 lt.134
  152.9 4.4 %collective-permute-done.1 = bf16[256,1152]{1,0:T(8,128)(2,1)} collective-permute-done((bf16[256,1152]{1,0:T(8,128)(2,1)S(1)}, bf16[256,1152]{1,0:T(8,128)(2,1)}, u32[]{:S(2)}, u32[]{:S(2)}) %collective-permute-start.1) | collective-permute-done | bytes 589856 | tf_op jit(solution)/shard_map/ppermute | solution.py:28
  157.3 1.0 slice.36
  158.3 1.9 collective-permute-start.3
  160.2 0.0 collective-permute-done.2
  160.2 1.0 slice.37
  161.2 5.3 %collective-permute-start.4 = (bf16[128,1152]{1,0:T(8,128)(2,1)S(1)}, bf16[128,1152]{1,0:T(8,128)(2,1)S(1)}, u32[]{:S(2)}, u32[]{:S(2)}) collective-permute-start(bf16[128,1152]{1,0:T(8,128)(2,1)S(1)} %slice.37), channel_id=1, source_target_pairs={{0,24},{8,0},{16,8},{24,16},{1,25},{9,1},{17,9},{25,17},{2,26},{10... | collective-permute-start | bytes 884744 | tf_op jit(solution)/shard_map/ppermute | solution.py:28
  166.5 1.1 constant_dynamic-update-slice_fusion.3
  167.7 1.2 constant_dynamic-update-slice_fusion.2
  168.9 0.0 collective-permute-done.3
  169.0 2.1 %collective-permute-done.4 = bf16[128,1152]{1,0:T(8,128)(2,1)S(1)} collective-permute-done((bf16[128,1152]{1,0:T(8,128)(2,1)S(1)}, bf16[128,1152]{1,0:T(8,128)(2,1)S(1)}, u32[]{:S(2)}, u32[]{:S(2)}) %collective-permute-start.4) | collective-permute-done | bytes 294944 | tf_op jit(solution)/shard_map/ppermute | solution.py:28
  171.2 0.5 fusion.2
  171.7 3.0 %convolution_convert_fusion = bf16[2,512,1152]{2,1,0:T(8,128)(2,1)S(1)} fusion(bf16[1024,1152]{1,0:T(8,128)(2,1)S(1)} %constant_dynamic-update-slice_fusion, f32[1024]{0:T(1024)S(1)} %maximum_convert_fusion.1, f32[1152]{0:T(1024)S(1)} %add_rsqrt_fusion, bf16[2,256,512]{1,2,0:T(8,128)(2,1)S(1)} %bitcast.78, bf16[2,256,512]{1,2,0:T(8,128)(2,1)S(1)} %bitcast.79, ...), kind=kOutput, calls=%fused_computation.12 | convolution fusion | flops 2430205952 | bytes 6824448 | tf_op jit(solution)/shard_map/dot_general | solution.py:115
  174.8 0.2 fusion.47
  175.0 5.2 %fusion.48 = (f32[4,256]{1,0:T(4,128)S(1)}, f32[4,256,1152]{1,2,0:T(8,128)}) fusion(bf16[4,128,1152]{2,1,0:T(8,128)(2,1)S(1)} %bitcast.77, pred[1152]{0:T(1024)(128)(4,1)S(1)} %lt.134, bf16[256,512]{1,0:T(8,128)(2,1)} %param.15), kind=kOutput, calls=%fused_computation.88 | convolution fusion | flops 306709632 | bytes 6165632 | tf_op jit(solution)/shard_map/sub | solution.py:128
  180.1 2.9 %fusion.21 = bf16[4,128,256]{2,1,0:T(8,128)(2,1)S(1)} fusion(bf16[4,128,1152]{2,1,0:T(8,128)(2,1)S(1)} %bitcast.76, f32[4,256,1152]{1,2,0:T(8,128)} %get-tuple-element.20, f32[4,256]{1,0:T(4,128)S(1)} %get-tuple-element.19), kind=kOutput, calls=%fused_computation.34 | convolution fusion | flops 304480256 | bytes 6164480 | tf_op jit(solution)/shard_map/htr,hdr->thd/dot_general | solution.py:130
  183.0 0.5 fusion.20
  183.5 23.4 %all_to_all.26 = bf16[32,8,1024]{2,1,0:T(8,128)(2,1)S(1)} all-to-all(bf16[32,8,1024]{2,1,0:T(8,128)(2,1)S(1)} %fusion.20), channel_id=1, replica_groups=mesh['y'=8,'core'=2,'x'=4,'z'=8] {'x','z'}, dimensions={0} | all-to-all | bytes 1048576 | tf_op jit(solution)/shard_map/all_to_all | solution.py:136
  206.9 0.7 reduce_sum.72
  (25 shorter events, 0.3 us)
Async XLA Ops:
  6.5 176.5 %copy-start = (bf16[512,1024]{1,0:T(8,128)(2,1)S(1)}, bf16[512,1024]{1,0:T(8,128)(2,1)}, u32[]{:S(2)}) copy-start(bf16[512,1024]{1,0:T(8,128)(2,1)} %param.16) | copy-start | bytes 3145732
  6.5 52.3 %copy-start.5 = (bf16[1024]{0:T(1024)(128)(2,1)S(1)}, bf16[1024]{0:T(1024)(128)(2,1)}, u32[]{:S(2)}) copy-start(bf16[1024]{0:T(1024)(128)(2,1)} %param.10) | copy-start | bytes 6148
  6.5 50.3 %all-gather.2.cloned.1.call-start = ((), (), s32[]{:S(2)}) async-start(), calls=%async_computation.5 | async-start | bytes 2359296 | tf_op jit(solution)/shard_map/all_gather | solution.py:63
  10.1 48.8 %all-to-all-start = ((bf16[32,32,384]{2,1,0:T(8,128)(2,1)}), bf16[32,32,384]{2,1,0:T(8,128)(2,1)S(1)}, u32[]{:S(2)}, u32[]{:S(2)}) async-start(bf16[32,32,384]{2,1,0:T(8,128)(2,1)} %broadcast_in_dim.26), calls=%async_computation | async-start | bytes 1572864 | tf_op jit(solution)/shard_map/all_to_all | solution.py:23
  56.9 6.4 %collective-permute-start = (bf16[512,2048]{1,0:T(8,128)(2,1)}, bf16[512,2048]{1,0:T(8,128)(2,1)}, u32[]{:S(2)}, u32[]{:S(2)}) collective-permute-start(bf16[512,2048]{1,0:T(8,128)(2,1)} %all-gather.2.cloned.1.call-done), channel_id=1, source_target_pairs={{0,32},{32,0},{1,33},{33,1},{2,34},{34,2},{3,35},{35,3},{4,36},{36... | collective-permute-start | bytes 6291464 | tf_op jit(solution)/shard_map/ppermute | solution.py:12
  58.9 1.6 copy-start.7
  67.9 11.3 %copy-start.4 = (s32[6144]{0:T(1024)S(1)}, s32[6144]{0:T(1024)}, u32[]{:S(2)}) copy-start(s32[6144]{0:T(1024)} %param.17) | copy-start | bytes 73732
  67.9 34.7 %copy-start.3 = (bf16[384,32]{0,1:T(8,128)(2,1)S(1)}, bf16[384,32]{0,1:T(8,128)(2,1)}, u32[]{:S(2)}) copy-start(bf16[384,32]{0,1:T(8,128)(2,1)} %param.9) | copy-start | bytes 73732
  68.9 33.6 %all-to-all-start.1 = ((bf16[32,32,384]{2,1,0:T(8,128)(2,1)}), bf16[32,32,384]{2,1,0:T(8,128)(2,1)S(1)}, u32[]{:S(2)}, u32[]{:S(2)}) async-start(bf16[32,32,384]{2,1,0:T(8,128)(2,1)} %bitcast.14), calls=%async_computation.1 | async-start | bytes 1572864 | tf_op jit(solution)/shard_map/all_to_all | solution.py:93
  117.0 22.3 %all-to-all-start.3 = ((bf16[8,32,1152]{2,1,0:T(8,128)(2,1)}), bf16[8,32,1152]{2,1,0:T(8,128)(2,1)S(1)}, u32[]{:S(2)}, u32[]{:S(2)}) async-start(bf16[8,32,1152]{2,1,0:T(8,128)(2,1)} %broadcast_in_dim.56), calls=%async_computation.3 | async-start | bytes 1179648 | tf_op jit(solution)/shard_map/all_to_all | solution.py:23
  121.1 27.9 %copy-start.6 = (bf16[1024]{0:T(1024)(128)(2,1)S(1)}, bf16[1024]{0:T(1024)(128)(2,1)}, u32[]{:S(2)}) copy-start(bf16[1024]{0:T(1024)(128)(2,1)} %param.13) | copy-start | bytes 6148
  139.4 17.9 %collective-permute-start.1 = (bf16[256,1152]{1,0:T(8,128)(2,1)S(1)}, bf16[256,1152]{1,0:T(8,128)(2,1)}, u32[]{:S(2)}, u32[]{:S(2)}) collective-permute-start(bf16[256,1152]{1,0:T(8,128)(2,1)S(1)} %bitcast.72), channel_id=1, source_target_pairs={{0,8},{8,16},{16,24},{24,0},{1,9},{9,17},{17,25},{25,1},{2,10},{10... | collective-permute-start | bytes 1769480 | tf_op jit(solution)/shard_map/ppermute | solution.py:28
  141.9 18.4 %collective-permute-start.2 = (bf16[256,1152]{1,0:T(8,128)(2,1)S(1)}, bf16[256,1152]{1,0:T(8,128)(2,1)}, u32[]{:S(2)}, u32[]{:S(2)}) collective-permute-start(bf16[256,1152]{1,0:T(8,128)(2,1)S(1)} %bitcast.73), channel_id=1, source_target_pairs={{0,24},{8,0},{16,8},{24,16},{1,25},{9,1},{17,9},{25,17},{2,26},{10... | collective-permute-start | bytes 1769480 | tf_op jit(solution)/shard_map/ppermute | solution.py:28
  158.3 10.7 %collective-permute-start.3 = (bf16[128,1152]{1,0:T(8,128)(2,1)S(1)}, bf16[128,1152]{1,0:T(8,128)(2,1)S(1)}, u32[]{:S(2)}, u32[]{:S(2)}) collective-permute-start(bf16[128,1152]{1,0:T(8,128)(2,1)S(1)} %slice.36), channel_id=1, source_target_pairs={{0,8},{8,16},{16,24},{24,0},{1,9},{9,17},{17,25},{25,1},{2,10},{10... | collective-permute-start | bytes 884744 | tf_op jit(solution)/shard_map/ppermute | solution.py:28
  161.2 9.9 %collective-permute-start.4 = (bf16[128,1152]{1,0:T(8,128)(2,1)S(1)}, bf16[128,1152]{1,0:T(8,128)(2,1)S(1)}, u32[]{:S(2)}, u32[]{:S(2)}) collective-permute-start(bf16[128,1152]{1,0:T(8,128)(2,1)S(1)} %slice.37), channel_id=1, source_target_pairs={{0,24},{8,0},{16,8},{24,16},{1,25},{9,1},{17,9},{25,17},{2,26},{10... | collective-permute-start | bytes 884744 | tf_op jit(solution)/shard_map/ppermute | solution.py:28
  167.7 4.0 %copy-start.1 = (bf16[2,1,256,512]{2,3,0,1:T(8,128)(2,1)S(1)}, bf16[2,1,256,512]{2,3,0,1:T(8,128)(2,1)}, u32[]{:S(2)}) copy-start(bf16[2,1,256,512]{2,3,0,1:T(8,128)(2,1)} %copy.74) | copy-start | bytes 1572868
  167.7 4.0 %copy-start.2 = (bf16[2,1,256,512]{2,3,0,1:T(8,128)(2,1)S(1)}, bf16[2,1,256,512]{2,3,0,1:T(8,128)(2,1)}, u32[]{:S(2)}) copy-start(bf16[2,1,256,512]{2,3,0,1:T(8,128)(2,1)} %copy.73) | copy-start | bytes 1572868
Sparse Core Ops, SparseCore 0:
  9.4 47.4 all-gather.1

commit v3 on v1

v3 whole, which is shorter than its diff:
```python
import jax
import jax.numpy as jnp
from jax import lax
from jax.experimental import pallas as pl
from jax.experimental.pallas import tpu as pltpu
from jax.sharding import Mesh, PartitionSpec as P

HEAD_DIM = 128
GRP = ("y", "core")
MDL = ("x", "z")


def swap_cores(value):
    return lax.ppermute(value, "core", [(0, 1), (1, 0)])


def spread(value, axes):
    copies = jnp.broadcast_to(value[None], (lax.axis_size(axes),) + value.shape)
    return lax.all_to_all(copies, axes, 0, 0, tiled=True).reshape(-1, value.shape[-1])


def shift(value, axis, step):
    size = lax.axis_size(axis)
    return lax.ppermute(value, axis, [(i, (i + step) % size) for i in range(size)])


def ring_gather(value, axis, beside):
    size = lax.axis_size(axis)
    blocks, steps = [value], [0]
    up = down = value
    for step in range(1, size // 2):
        up, down = shift(up, axis, 1), shift(down, axis, -1)
        blocks += [up, down]
        steps += [size - step, step]
    up, beside = lax.optimization_barrier((up, beside))
    blocks.append(shift(up, axis, 1))
    steps.append(size // 2)
    return blocks, steps, beside


def slot_plan(row_question, rows_local, groups, my_group):
    capacity = 3 * rows_local // groups
    owners = row_question.reshape(groups, rows_local)
    questions = jnp.arange(groups, dtype=jnp.int32)
    counts = jnp.sum((owners[:, :, None] == questions).astype(jnp.int32), axis=1)
    slots = jnp.arange(capacity, dtype=jnp.int32)
    mine = lax.dynamic_index_in_dim(owners, my_group, 0, keepdims=False)
    sent_counts = lax.dynamic_index_in_dim(counts, my_group, 0, keepdims=False)
    sent_starts = jnp.sum((mine[None, :] < questions[:, None]).astype(jnp.int32), axis=1)
    source = jnp.where(
        slots[None, :] < sent_counts[:, None], sent_starts[:, None] + slots[None, :], -1
    )
    got_counts = lax.dynamic_index_in_dim(counts, my_group, 1, keepdims=False)
    got_valid = (slots[None, :] < got_counts[:, None]).reshape(-1)
    rows = jnp.arange(rows_local, dtype=jnp.int32)
    pick = (rows[:, None] == source.reshape(1, -1)).astype(jnp.bfloat16)
    return capacity, pick, got_valid


def ffn_kernel(order_ref, core_ref, rows_ref, gain_ref, own_ref, other_ref, out_ref, normed, own_rows, other_rows, hidden):
    width, columns = rows_ref.shape
    piece = own_ref.shape[0] // order_ref.shape[0]
    hid = hidden.shape[1]
    wide = rows_ref[...].astype(jnp.float32)
    factor = lax.rsqrt(jnp.sum(wide * wide, axis=0, keepdims=True) * (1.0 / width) + 1e-06)
    normed[...] = (wide * factor * gain_ref[...]).astype(jnp.bfloat16)
    core = core_ref[0]
    for spot in range(order_ref.shape[0]):
        base = order_ref[spot] * (2 * piece)
        mine = pl.multiple_of(base + core * piece, piece)
        theirs = pl.multiple_of(base + (1 - core) * piece, piece)
        own_rows[spot * piece : (spot + 1) * piece, :] = normed[pl.ds(mine, piece), :]
        other_rows[spot * piece : (spot + 1) * piece, :] = normed[pl.ds(theirs, piece), :]
    over_first = (((0,), (0,)), ((), ()))
    over_last = (((1,), (1,)), ((), ()))
    for start in range(0, hid, 256):
        part = lax.dot_general(
            own_rows[...], own_ref[:, start : start + 256], over_first,
            preferred_element_type=jnp.float32,
        ) + lax.dot_general(
            other_rows[...], other_ref[:, start : start + 256], over_first,
            preferred_element_type=jnp.float32,
        )
        hidden[:, start : start + 256] = jnp.maximum(part, 0.0).astype(jnp.bfloat16)
    for weight_ref, shift_by in ((own_ref, core), (other_ref, 1 - core)):
        share = lax.dot_general(
            weight_ref[:, hid:], hidden[...], over_last, preferred_element_type=jnp.float32
        ).astype(jnp.bfloat16)
        for spot in range(order_ref.shape[0]):
            at = pl.multiple_of(order_ref[spot] * (2 * piece) + shift_by * piece, piece)
            out_ref[pl.ds(at, piece), :] = share[spot * piece : (spot + 1) * piece, :]


def ffn_shares(order, core, rows, gain, own, other):
    width, columns = rows.shape
    hid = own.shape[1] // 2
    smem = pl.BlockSpec(memory_space=pltpu.SMEM)
    vmem = pl.BlockSpec(memory_space=pltpu.VMEM)
    return pl.pallas_call(
        ffn_kernel,
        out_shape=jax.ShapeDtypeStruct((width, columns), jnp.bfloat16),
        in_specs=[smem, smem, vmem, vmem, vmem, vmem],
        out_specs=vmem,
        scratch_shapes=[
            pltpu.VMEM((width, columns), jnp.bfloat16),
            pltpu.VMEM((width // 2, columns), jnp.bfloat16),
            pltpu.VMEM((width // 2, columns), jnp.bfloat16),
            pltpu.VMEM((columns, hid), jnp.bfloat16),
        ],
        cost_estimate=pl.CostEstimate(
            flops=4 * width * hid * columns, transcendentals=columns, bytes_accessed=12 << 20
        ),
        name="ffn_shares",
    )(order, core, rows, gain, own, other)


def attend_kernel(
    order_ref, near_ref, behind_ref, ahead_ref, low_ref, high_ref, kv_ref, q_ref, out_w_ref,
    valid_ref, out_ref, total, factor_ref,
):
    head = pl.program_id(0)
    quarter, slots = near_ref.shape
    half = quarter // 2
    width = 4 * quarter

    @pl.when(head == 0)
    def _():
        squares = jnp.zeros((1, slots), jnp.float32)
        for ref in (near_ref, behind_ref, ahead_ref, low_ref, high_ref):
            wide = ref[...].astype(jnp.float32)
            squares += jnp.sum(wide * wide, axis=0, keepdims=True)
        factor_ref[...] = lax.rsqrt(squares * (1.0 / width) + 1e-06)

    near_at = pl.multiple_of(order_ref[0] * quarter, quarter)
    behind_at = pl.multiple_of(order_ref[1] * quarter, quarter)
    ahead_at = pl.multiple_of(order_ref[2] * quarter, quarter)
    low_at = pl.multiple_of(order_ref[3] * quarter, quarter)
    high_at = pl.multiple_of(order_ref[3] * quarter + half, half)

    def project(kind):
        parts = [
            jnp.dot(kv_ref[kind, :, pl.ds(at, size)], ref[...], preferred_element_type=jnp.float32)
            for ref, at, size in (
                (near_ref, near_at, quarter),
                (behind_ref, behind_at, quarter),
                (ahead_ref, ahead_at, quarter),
                (low_ref, low_at, half),
                (high_ref, high_at, half),
            )
        ]
        whole = parts[0] + parts[1] + parts[2] + parts[3] + parts[4]
        return (whole * factor_ref[...]).astype(jnp.bfloat16)

    scores = jnp.dot(q_ref[...], project(0), preferred_element_type=jnp.float32)
    valid = valid_ref[...] > 0.0
    scores = jnp.where(valid, scores, -1e30)
    top = jnp.max(scores, axis=-1, keepdims=True)
    raised = jnp.where(valid, jnp.exp(scores - top), 0.0)
    weight = 1.0 / jnp.sum(raised, axis=-1, keepdims=True)
    probabilities = (raised * weight).astype(jnp.bfloat16)
    attended = lax.dot_general(
        probabilities, project(1), (((1,), (1,)), ((), ())), preferred_element_type=jnp.float32
    ).astype(jnp.bfloat16)
    share = jnp.dot(attended, out_w_ref[...], preferred_element_type=jnp.float32)

    @pl.when(head == 0)
    def _():
        total[...] = share

    @pl.when(head > 0)
    def _():
        total[...] += share

    @pl.when(head == pl.num_programs(0) - 1)
    def _():
        out_ref[...] = total[...].astype(jnp.bfloat16)


def attend(order, near, behind, ahead, low, high, kv_rows, queries, attn_out, valid):
    targets, head_cols = queries.shape
    heads = head_cols // HEAD_DIM
    quarter, slots = near.shape
    width = attn_out.shape[1]

    def whole(array):
        return pl.BlockSpec(array.shape, lambda h: (0,) * array.ndim, pipeline_mode=pl.Buffered(1))

    return pl.pallas_call(
        attend_kernel,
        grid=(heads,),
        out_shape=jax.ShapeDtypeStruct((targets, width), jnp.bfloat16),
        in_specs=[
            pl.BlockSpec(memory_space=pltpu.SMEM),
            *[whole(array) for array in (near, behind, ahead, low, high)],
            pl.BlockSpec((2, HEAD_DIM, kv_rows.shape[2]), lambda h: (0, h, 0)),
            pl.BlockSpec((targets, HEAD_DIM), lambda h: (0, h)),
            pl.BlockSpec((HEAD_DIM, width), lambda h: (h, 0)),
            whole(valid),
        ],
        out_specs=pl.BlockSpec((targets, width), lambda h: (0, 0)),
        scratch_shapes=[
            pltpu.VMEM((targets, width), jnp.float32),
            pltpu.VMEM((1, slots), jnp.float32),
        ],
        compiler_params=pltpu.CompilerParams(dimension_semantics=("arbitrary",)),
        cost_estimate=pl.CostEstimate(
            flops=4 * slots * width * head_cols + 4 * slots * targets * head_cols,
            transcendentals=targets * slots * heads,
            bytes_accessed=6 << 20,
        ),
        name="attend",
    )(order, near, behind, ahead, low, high, kv_rows, queries, attn_out, valid)


def local(
    row_states, ffn_gain, ffn_in, ffn_out, final_gain, kv_weight, queries, attn_out, row_question
):
    groups = lax.axis_size(GRP)
    models = lax.axis_size(MDL)
    my_group = lax.axis_index(GRP)
    my_core = lax.axis_index("core")
    rows_local, feats_local = row_states.shape
    width = feats_local * models

    own_rows = row_states.T
    both = jnp.concatenate([ffn_in, ffn_out.T], axis=1)
    blocks, steps, full_rows = ring_gather(both, "y", spread(own_rows, MDL))
    both_half = jnp.concatenate(blocks, axis=0)
    both_other = swap_cores(both_half)
    y_size = lax.axis_size("y")
    y_order = (lax.axis_index("y") + jnp.array(steps, jnp.int32)) % y_size
    shares = ffn_shares(
        y_order,
        my_core.reshape(1),
        full_rows,
        ffn_gain.astype(jnp.float32)[:, None],
        both_half,
        both_other,
    ).reshape(models, feats_local, rows_local)
    arrived = lax.all_to_all(shares, MDL, 0, 0, tiled=True)
    ffn_sum = jnp.sum(arrived.astype(jnp.float32), axis=0)
    enc_state = (own_rows.astype(jnp.float32) + ffn_sum).astype(jnp.bfloat16)

    capacity, pick, got_valid = slot_plan(row_question, rows_local, groups, my_group)
    packed = jnp.dot(enc_state, pick, preferred_element_type=jnp.float32).astype(jnp.bfloat16)
    packed = packed.reshape(feats_local, groups, capacity).transpose(1, 0, 2)
    regrouped = lax.all_to_all(packed, GRP, 0, 0, tiled=True)
    slots = regrouped.transpose(1, 0, 2).reshape(feats_local, groups * capacity)
    near = spread(slots, "z")
    behind, ahead = shift(near, "x", 1), shift(near, "x", -1)
    half = near.shape[0] // 2
    far_low, far_high = shift(behind[:half], "x", 1), shift(ahead[half:], "x", -1)
    x_order = (lax.axis_index("x") + jnp.array([0, 3, 1, 2], jnp.int32)) % lax.axis_size("x")
    gained = kv_weight.astype(jnp.float32) * final_gain.astype(jnp.float32)[None, :, None]
    kv_rows = gained.astype(jnp.bfloat16).transpose(0, 2, 1)
    partial = attend(
        x_order,
        near,
        behind,
        ahead,
        far_low,
        far_high,
        kv_rows,
        queries,
        attn_out,
        got_valid.astype(jnp.float32)[None, :],
    )
    partial = partial.reshape(models, queries.shape[0] // models, width)
    shares_out = lax.all_to_all(partial, MDL, 0, 0, tiled=True)
    return jnp.sum(shares_out.astype(jnp.float32), axis=0).astype(jnp.bfloat16)


def solution(mesh):
    fine = Mesh(mesh.devices.reshape(-1, 2, 4, 8), ("y", "core", "x", "z"))
    in_specs = (
        P(GRP, MDL),
        P(),
        P(GRP, MDL),
        P(MDL, GRP),
        P(),
        P(None, None, MDL),
        P(GRP, MDL),
        P(MDL, None),
        P(),
    )
    out_specs = P(GRP + MDL, None)
    return jax.shard_map(local, mesh=fine, in_specs=in_specs, out_specs=out_specs, check_vma=False)
```

time: 276 us -> 206 us (0.75)
  waiting for transfers between devices: 130 us -> 49.4 us
  starting transfers between devices: 14.4 us -> 61.8 us
  blocking collectives: 88 us -> 60.2 us
  Pallas kernels: 0 us -> 17.7 us
  matrix products: 17.7 us -> 0.42 us
  between operations: 13.4 us -> 0.4 us
  local copies, waits for them, and re-layouts: 5.66 us -> 10.9 us
    all_gather x3 -> x0, waiting for transfers between devices: 106 us -> none  [the longest x1 75.7 us: local(): slot_rows = lax.all_gather(slots, MDL, axis=0, tiled=True)]
    all_gather x1 -> x0, blocking collectives: 54.6 us -> none  [local(): full_rows = lax.all_gather(own_rows, MDL, axis=0, tiled=True)]
    ppermute x0 -> x11, starting transfers between devices: none -> 37.4 us  [shift(): lax.ppermute(value, axis, [(i, (i + step) % size) for i in range(size)])]
    ppermute x0 -> x11, waiting for transfers between devices: none -> 24.2 us  [shift(): lax.ppermute(value, axis, [(i, (i + step) % size) for i in range(size)])]
    all_to_all x0 -> x1, blocking collectives: none -> 22.1 us  [spread(): lax.all_to_all(copies, axes, 0, 0, tiled=True).reshape(-1, value.shape[-1])]
    pallas_call x0 -> x2, Pallas kernels: none -> 17.7 us  [the longest x1 11.7 us: attend(): pl.pallas_call(attend_kernel, grid=(heads,), out_shape=jax.ShapeDtypeStru...]
    all_to_all x0 -> x1, starting transfers between devices: none -> 12.6 us  [spread(): lax.all_to_all(copies, axes, 0, 0, tiled=True).reshape(-1, value.shape[-1])]
    dot_general x7 -> x0, matrix products: 11.8 us -> none  [the longest x1 3.45 us: local(): lax.dot_general(kv_weight, encoded, (((1,), (0,)), ((), ())), preferred_e...]
  transfers between devices with their start and end apart: 6 -> 14, of which waited for: 3 -> 9; matrix products, arithmetic and copies ran while one was open for 3% -> 5% of each run, Pallas kernels for 0% -> 0%
where the time goes in v3:
time: 206 us; the launch traced here: 205 us
  starting transfers between devices  61.8 us (30%)
  blocking collectives  60.2 us (29%)
  waiting for transfers between devices  49.4 us (24%)
  Pallas kernels  17.7 us (9%)
  local copies, waits for them, and re-layouts  10.9 us (5%)
  other arithmetic  4.54 us (2%)
    ppermute x11, starting transfers between devices, shift(): lax.ppermute(value, axis, [(i, (i + step) % size) for i in range(size)])  37.4 us
    ppermute x11, waiting for transfers between devices, shift(): lax.ppermute(value, axis, [(i, (i + step) % size) for i in range(size)])  24.2 us
    all_to_all x1, blocking collectives, local(): shares_out = lax.all_to_all(partial, MDL, 0, 0, tiled=True)  23.3 us
    all_to_all x1, waiting for transfers between devices, local(): arrived = lax.all_to_all(shares, MDL, 0, 0, tiled=True)  22.5 us
    all_to_all x1, blocking collectives, spread(): lax.all_to_all(copies, axes, 0, 0, tiled=True).reshape(-1, value.shape[-1])  22.1 us
    all_to_all x1, blocking collectives, local(): regrouped = lax.all_to_all(packed, GRP, 0, 0, tiled=True)  14.8 us
    all_to_all x1, starting transfers between devices, spread(): lax.all_to_all(copies, axes, 0, 0, tiled=True).reshape(-1, value.shape[-1])  12.6 us
    pallas_call x1, Pallas kernels, attend(): pl.pallas_call(attend_kernel, grid=(heads,), out_shape=jax.ShapeDtypeStru...  11.7 us
  transfers between devices with their start and end apart: 14, of which 9 were waited for; matrix products, arithmetic and copies ran while one was open for 5% of the time, Pallas kernels for 0%

profile of v3, /device:TPU:64, one launch (start us, length us, event | category | flops | bytes accessed | tf_op | source)
XLA Modules:
  0.0 205.3 jit_solution(2362576150948636960)
XLA Ops:
  0.0 1.7 broadcast_in_dim.14
  1.8 12.6 %all-to-all-start = ((bf16[32,32,384]{2,1,0:T(8,128)(2,1)}), bf16[32,32,384]{2,1,0:T(8,128)(2,1)S(1)}, u32[]{:S(2)}, u32[]{:S(2)}) async-start(bf16[32,32,384]{2,1,0:T(8,128)(2,1)} %broadcast_in_dim.14), calls=%async_computation | async-start | bytes 1572864 | tf_op jit(solution)/shard_map/all_to_all | solution.py:19
  14.3 0.0 copy-done.4
  14.4 0.0 copy-done.5
  14.4 0.0 copy-start.8
  14.4 3.5 %collective-permute-start = (bf16[64,2048]{1,0:T(8,128)(2,1)S(1)}, bf16[64,2048]{1,0:T(8,128)(2,1)S(1)}, u32[]{:S(2)}, u32[]{:S(2)}) collective-permute-start(bf16[64,2048]{1,0:T(8,128)(2,1)S(1)} %get-tuple-element.10), channel_id=1, source_target_pairs={{0,64},{64,128},{128,192},{192,256},{256,320},{320,384},{384,448},... | collective-permute-start | bytes 786440 | tf_op jit(solution)/shard_map/ppermute | solution.py:24
  17.9 3.8 %collective-permute-start.3 = (bf16[64,2048]{1,0:T(8,128)(2,1)S(1)}, bf16[64,2048]{1,0:T(8,128)(2,1)S(1)}, u32[]{:S(2)}, u32[]{:S(2)}) collective-permute-start(bf16[64,2048]{1,0:T(8,128)(2,1)S(1)} %get-tuple-element.10), channel_id=1, source_target_pairs={{0,448},{64,0},{128,64},{192,128},{256,192},{320,256},{384,320},{4... | collective-permute-start | bytes 786440 | tf_op jit(solution)/shard_map/ppermute | solution.py:24
  21.7 3.8 %collective-permute-done = bf16[64,2048]{1,0:T(8,128)(2,1)S(1)} collective-permute-done((bf16[64,2048]{1,0:T(8,128)(2,1)S(1)}, bf16[64,2048]{1,0:T(8,128)(2,1)S(1)}, u32[]{:S(2)}, u32[]{:S(2)}) %collective-permute-start) | collective-permute-done | bytes 262176 | tf_op jit(solution)/shard_map/ppermute | solution.py:24
  25.5 1.9 collective-permute-start.1
  27.5 0.0 copy-start.13
  27.5 0.0 collective-permute-done.3
  27.5 5.1 %collective-permute-start.4 = (bf16[64,2048]{1,0:T(8,128)(2,1)S(1)}, bf16[64,2048]{1,0:T(8,128)(2,1)S(1)}, u32[]{:S(2)}, u32[]{:S(2)}) collective-permute-start(bf16[64,2048]{1,0:T(8,128)(2,1)S(1)} %collective-permute-done.3), channel_id=1, source_target_pairs={{0,448},{64,0},{128,64},{192,128},{256,192},{320,256},{384,320},{4... | collective-permute-start | bytes 786440 | tf_op jit(solution)/shard_map/ppermute | solution.py:24
  32.7 2.9 %collective-permute-done.1 = bf16[64,2048]{1,0:T(8,128)(2,1)S(1)} collective-permute-done((bf16[64,2048]{1,0:T(8,128)(2,1)S(1)}, bf16[64,2048]{1,0:T(8,128)(2,1)S(1)}, u32[]{:S(2)}, u32[]{:S(2)}) %collective-permute-start.1) | collective-permute-done | bytes 262176 | tf_op jit(solution)/shard_map/ppermute | solution.py:24
  35.5 1.9 collective-permute-start.2
  37.5 0.0 collective-permute-done.4
  37.5 5.1 %collective-permute-start.5 = (bf16[64,2048]{1,0:T(8,128)(2,1)S(1)}, bf16[64,2048]{1,0:T(8,128)(2,1)}, u32[]{:S(2)}, u32[]{:S(2)}) collective-permute-start(bf16[64,2048]{1,0:T(8,128)(2,1)S(1)} %collective-permute-done.4), channel_id=1, source_target_pairs={{0,448},{64,0},{128,64},{192,128},{256,192},{320,256},{384,320},{4... | collective-permute-start | bytes 786440 | tf_op jit(solution)/shard_map/ppermute | solution.py:24
  42.7 2.3 %collective-permute-done.2 = bf16[64,2048]{1,0:T(8,128)(2,1)S(1)} collective-permute-done((bf16[64,2048]{1,0:T(8,128)(2,1)S(1)}, bf16[64,2048]{1,0:T(8,128)(2,1)S(1)}, u32[]{:S(2)}, u32[]{:S(2)}) %collective-permute-start.2) | collective-permute-done | bytes 262176 | tf_op jit(solution)/shard_map/ppermute | solution.py:24
  45.0 0.0 all-to-all-done
  45.0 1.9 collective-permute-start.6
  47.0 0.0 collective-permute-done.5
  47.0 1.0 constant_dynamic-update-slice_fusion.1
  47.9 6.5 %collective-permute-done.6 = bf16[64,2048]{1,0:T(8,128)(2,1)S(1)} collective-permute-done((bf16[64,2048]{1,0:T(8,128)(2,1)S(1)}, bf16[64,2048]{1,0:T(8,128)(2,1)S(1)}, u32[]{:S(2)}, u32[]{:S(2)}) %collective-permute-start.6) | collective-permute-done | bytes 262176 | tf_op jit(solution)/shard_map/ppermute | solution.py:24
  54.5 0.0 copy-start.1
  54.5 1.9 collective-permute-start.7
  56.4 0.0 copy-done.8
  56.5 1.0 copy.26.gain_ref
  57.5 0.0 copy-done.13
  57.5 0.6 and_select_fusion.order_ref
  58.1 2.6 %collective-permute-done.7.other_ref = bf16[512,2048]{1,0:T(8,128)(2,1)} collective-permute-done((bf16[512,2048]{1,0:T(8,128)(2,1)S(1)}, bf16[512,2048]{1,0:T(8,128)(2,1)}, u32[]{:S(2)}, u32[]{:S(2)}) %collective-permute-start.7) | collective-permute-done | bytes 2097184 | tf_op jit(solution)/shard_map/ppermute | solution.py:14
  60.7 0.0 copy-done
  60.7 6.0 %ffn_shares.1 = bf16[1024,384]{1,0:T(8,128)(2,1)} custom-call(s32[8]{0:T(128)} %and_select_fusion.order_ref, s32[1]{0:T(128)} %bitcast.1.core_ref, bf16[1024,384]{1,0:T(8,128)(2,1)} %bitcast.20, f32[1024,1]{1,0:T(8,128)} %copy.26.gain_ref, bf16[512,2048]{1,0:T(8,128)(2,1)} %copy-done.1, bf16[512,2048]{1,0:T(8,128)(2,1)} %collective-permute-done.7.other_ref), custom_call_target="tpu_custom_call" | custom-call | flops 1610612736 | bytes 12582912 | tf_op jit(solution)/shard_map/ffn_shares/pallas_call | solution.py:99
  66.7 9.9 %all-to-all-start.1 = ((bf16[32,32,384]{2,1,0:T(8,128)(2,1)}), bf16[32,32,384]{2,1,0:T(8,128)(2,1)S(1)}, u32[]{:S(2)}, u32[]{:S(2)}) async-start(bf16[32,32,384]{2,1,0:T(8,128)(2,1)} %bitcast.21), calls=%async_computation.1 | async-start | bytes 1572864 | tf_op jit(solution)/shard_map/all_to_all | solution.py:240
  76.7 0.4 convert_reduce_fusion.1
  77.1 0.1 convert_reduce_fusion.2
  77.2 0.1 add_select_fusion
  77.3 0.1 select_n.36
  77.3 22.5 %all-to-all-done.1 = bf16[32,32,384]{2,1,0:T(8,128)(2,1)S(1)} async-done(((bf16[32,32,384]{2,1,0:T(8,128)(2,1)}), bf16[32,32,384]{2,1,0:T(8,128)(2,1)S(1)}, u32[]{:S(2)}, u32[]{:S(2)}) %all-to-all-start.1) | async-done | bytes 786464 | tf_op jit(solution)/shard_map/all_to_all | solution.py:240
  99.9 0.1 convert_reduce_fusion
  100.0 0.4 convolution_convert_fusion
  100.4 0.2 reshape.87
  100.7 14.8 %all_to_all.25 = bf16[16,32,72]{2,1,0:T(8,128)(2,1)S(1)} all-to-all(bf16[16,32,72]{2,1,0:T(8,128)(2,1)S(1)} %bitcast.26), channel_id=1, replica_groups=mesh['y'=8,'core'=2,'x'=4,'z'=8] {'y','core'}, dimensions={0} | all-to-all | bytes 147456 | tf_op jit(solution)/shard_map/all_to_all | solution.py:247
  115.6 0.1 copy.28
  115.6 0.2 broadcast_in_dim.18
  115.8 22.1 %all_to_all.26 = bf16[8,32,1152]{2,1,0:T(8,128)(2,1)S(1)} all-to-all(bf16[8,32,1152]{2,1,0:T(8,128)(2,1)S(1)} %broadcast_in_dim.19), channel_id=1, replica_groups=mesh['y'=8,'core'=2,'x'=4,'z'=8] {'z'}, dimensions={0} | all-to-all | bytes 1179648 | tf_op jit(solution)/shard_map/all_to_all | solution.py:19
  138.0 2.5 %collective-permute-start.8 = (bf16[256,1152]{1,0:T(8,128)(2,1)S(1)}, bf16[256,1152]{1,0:T(8,128)(2,1)S(1)}, u32[]{:S(2)}, u32[]{:S(2)}) collective-permute-start(bf16[256,1152]{1,0:T(8,128)(2,1)S(1)} %bitcast.22), channel_id=1, source_target_pairs={{0,8},{8,16},{16,24},{24,0},{1,9},{9,17},{17,25},{25,1},{2,10},{10... | collective-permute-start | bytes 1769480 | tf_op jit(solution)/shard_map/ppermute | solution.py:24
  140.5 4.5 %collective-permute-start.9 = (bf16[256,1152]{1,0:T(8,128)(2,1)S(1)}, bf16[256,1152]{1,0:T(8,128)(2,1)}, u32[]{:S(2)}, u32[]{:S(2)}) collective-permute-start(bf16[256,1152]{1,0:T(8,128)(2,1)S(1)} %bitcast.23), channel_id=1, source_target_pairs={{0,24},{8,0},{16,8},{24,16},{1,25},{9,1},{17,9},{25,17},{2,26},{10... | collective-permute-start | bytes 1769480 | tf_op jit(solution)/shard_map/ppermute | solution.py:24
  145.0 0.2 dynamic-slice_reduce_fusion
  145.2 0.1 fusion.2
  145.3 0.7 reshape.91.valid_ref
  146.0 3.0 %copy.29 = bf16[2,1024,512]{1,2,0:T(8,128)(2,1)S(1)} copy(bf16[2,1024,512]{2,1,0:T(8,128)(2,1)} %param.16) | data formatting | bytes 4194304 | tf_op args[5]
  149.0 0.6 and_select_fusion.1.order_ref
  149.6 6.3 %collective-permute-done.8.behind_ref = bf16[256,1152]{1,0:T(8,128)(2,1)S(1)} collective-permute-done((bf16[256,1152]{1,0:T(8,128)(2,1)S(1)}, bf16[256,1152]{1,0:T(8,128)(2,1)S(1)}, u32[]{:S(2)}, u32[]{:S(2)}) %collective-permute-start.8) | collective-permute-done | bytes 589856 | tf_op jit(solution)/shard_map/ppermute | solution.py:24
  156.0 1.9 collective-permute-start.10
  157.9 0.0 collective-permute-done.9.ahead_ref
  157.9 1.0 slice.9
  158.9 5.1 %collective-permute-start.11 = (bf16[128,1152]{1,0:T(8,128)(2,1)S(1)}, bf16[128,1152]{1,0:T(8,128)(2,1)S(1)}, u32[]{:S(2)}, u32[]{:S(2)}) collective-permute-start(bf16[128,1152]{1,0:T(8,128)(2,1)S(1)} %slice.9), channel_id=1, source_target_pairs={{0,24},{8,0},{16,8},{24,16},{1,25},{9,1},{17,9},{25,17},{2,26},{10... | collective-permute-start | bytes 884744 | tf_op jit(solution)/shard_map/ppermute | solution.py:24
  164.1 1.9 fusion.kv_ref
  166.0 0.8 collective-permute-done.10.low_ref
  166.8 0.7 copy-done.10
  167.5 1.5 collective-permute-done.11.high_ref
  169.0 0.7 copy-done.11
  169.7 11.7 %attend.1 = bf16[256,1024]{1,0:T(8,128)(2,1)} custom-call(s32[4]{0:T(128)} %and_select_fusion.1.order_ref, bf16[256,1152]{1,0:T(8,128)(2,1)} %bitcast.24, bf16[256,1152]{1,0:T(8,128)(2,1)} %copy-done.3, bf16[256,1152]{1,0:T(8,128)(2,1)} %collective-permute-done.9.ahead_ref, bf16[128,1152]{1,0:T(8,128)(2,1)} %copy-done.10, bf16[128,1152]{1,0:T(8,128)(2,1)} %copy-done.11, ...), custom_call_target="tpu_custom_call" | custom-call | flops 3019898880 | bytes 6291456 | tf_op jit(solution)/shard_map/attend/pallas_call | solution.py:188
  181.4 23.3 %all_to_all.27 = bf16[32,8,1024]{2,1,0:T(8,128)(2,1)S(1)} all-to-all(bf16[32,8,1024]{2,1,0:T(8,128)(2,1)} %bitcast.25), channel_id=1, replica_groups=mesh['y'=8,'core'=2,'x'=4,'z'=8] {'x','z'}, dimensions={0} | all-to-all | bytes 1048576 | tf_op jit(solution)/shard_map/all_to_all | solution.py:269
  204.6 0.7 reduce_sum.42
  (33 shorter events, 0.3 us)
Async XLA Ops:
  0.0 14.3 %copy-start.4 = (bf16[1024,64]{0,1:T(8,128)(2,1)S(1)}, bf16[1024,64]{0,1:T(8,128)(2,1)}, u32[]{:S(2)}) copy-start(bf16[1024,64]{0,1:T(8,128)(2,1)} %param.14) | copy-start | bytes 393220
  0.0 14.4 %copy-start.5 = (bf16[64,1024]{1,0:T(8,128)(2,1)S(1)}, bf16[64,1024]{1,0:T(8,128)(2,1)}, u32[]{:S(2)}) copy-start(bf16[64,1024]{1,0:T(8,128)(2,1)} %param.13) | copy-start | bytes 393220
  1.8 43.3 %all-to-all-start = ((bf16[32,32,384]{2,1,0:T(8,128)(2,1)}), bf16[32,32,384]{2,1,0:T(8,128)(2,1)S(1)}, u32[]{:S(2)}, u32[]{:S(2)}) async-start(bf16[32,32,384]{2,1,0:T(8,128)(2,1)} %broadcast_in_dim.14), calls=%async_computation | async-start | bytes 1572864 | tf_op jit(solution)/shard_map/all_to_all | solution.py:19
  14.4 42.1 %copy-start.8 = (bf16[1024]{0:T(1024)(128)(2,1)S(1)}, bf16[1024]{0:T(1024)(128)(2,1)}, u32[]{:S(2)}) copy-start(bf16[1024]{0:T(1024)(128)(2,1)} %param.12) | copy-start | bytes 6148
  14.4 11.1 %collective-permute-start = (bf16[64,2048]{1,0:T(8,128)(2,1)S(1)}, bf16[64,2048]{1,0:T(8,128)(2,1)S(1)}, u32[]{:S(2)}, u32[]{:S(2)}) collective-permute-start(bf16[64,2048]{1,0:T(8,128)(2,1)S(1)} %get-tuple-element.10), channel_id=1, source_target_pairs={{0,64},{64,128},{128,192},{192,256},{256,320},{320,384},{384,448},... | collective-permute-start | bytes 786440 | tf_op jit(solution)/shard_map/ppermute | solution.py:24
  17.9 9.6 %collective-permute-start.3 = (bf16[64,2048]{1,0:T(8,128)(2,1)S(1)}, bf16[64,2048]{1,0:T(8,128)(2,1)S(1)}, u32[]{:S(2)}, u32[]{:S(2)}) collective-permute-start(bf16[64,2048]{1,0:T(8,128)(2,1)S(1)} %get-tuple-element.10), channel_id=1, source_target_pairs={{0,448},{64,0},{128,64},{192,128},{256,192},{320,256},{384,320},{4... | collective-permute-start | bytes 786440 | tf_op jit(solution)/shard_map/ppermute | solution.py:24
  25.5 10.0 %collective-permute-start.1 = (bf16[64,2048]{1,0:T(8,128)(2,1)S(1)}, bf16[64,2048]{1,0:T(8,128)(2,1)S(1)}, u32[]{:S(2)}, u32[]{:S(2)}) collective-permute-start(bf16[64,2048]{1,0:T(8,128)(2,1)S(1)} %collective-permute-done), channel_id=1, source_target_pairs={{0,64},{64,128},{128,192},{192,256},{256,320},{320,384},{384,448},... | collective-permute-start | bytes 786440 | tf_op jit(solution)/shard_map/ppermute | solution.py:24
  27.5 30.0 %copy-start.13 = (s32[8]{0:T(128)S(1)}, s32[8]{0:T(128)}, u32[]{:S(2)}) copy-start(s32[8]{0:T(128)} %constant.71.clone) | copy-start | bytes 100
  27.5 10.0 %collective-permute-start.4 = (bf16[64,2048]{1,0:T(8,128)(2,1)S(1)}, bf16[64,2048]{1,0:T(8,128)(2,1)S(1)}, u32[]{:S(2)}, u32[]{:S(2)}) collective-permute-start(bf16[64,2048]{1,0:T(8,128)(2,1)S(1)} %collective-permute-done.3), channel_id=1, source_target_pairs={{0,448},{64,0},{128,64},{192,128},{256,192},{320,256},{384,320},{4... | collective-permute-start | bytes 786440 | tf_op jit(solution)/shard_map/ppermute | solution.py:24
  35.5 9.5 %collective-permute-start.2 = (bf16[64,2048]{1,0:T(8,128)(2,1)S(1)}, bf16[64,2048]{1,0:T(8,128)(2,1)S(1)}, u32[]{:S(2)}, u32[]{:S(2)}) collective-permute-start(bf16[64,2048]{1,0:T(8,128)(2,1)S(1)} %collective-permute-done.1), channel_id=1, source_target_pairs={{0,64},{64,128},{128,192},{192,256},{256,320},{320,384},{384,448},... | collective-permute-start | bytes 786440 | tf_op jit(solution)/shard_map/ppermute | solution.py:24
  37.5 9.5 %collective-permute-start.5 = (bf16[64,2048]{1,0:T(8,128)(2,1)S(1)}, bf16[64,2048]{1,0:T(8,128)(2,1)}, u32[]{:S(2)}, u32[]{:S(2)}) collective-permute-start(bf16[64,2048]{1,0:T(8,128)(2,1)S(1)} %collective-permute-done.4), channel_id=1, source_target_pairs={{0,448},{64,0},{128,64},{192,128},{256,192},{320,256},{384,320},{4... | collective-permute-start | bytes 786440 | tf_op jit(solution)/shard_map/ppermute | solution.py:24
  45.0 15.7 %copy-start = (bf16[32,32,384]{2,1,0:T(8,128)(2,1)}, bf16[32,32,384]{2,1,0:T(8,128)(2,1)S(1)}, u32[]{:S(2)}) copy-start(bf16[32,32,384]{2,1,0:T(8,128)(2,1)S(1)} %all-to-all-done) | copy-start | bytes 2359300
  45.0 9.5 %collective-permute-start.6 = (bf16[64,2048]{1,0:T(8,128)(2,1)S(1)}, bf16[64,2048]{1,0:T(8,128)(2,1)S(1)}, u32[]{:S(2)}, u32[]{:S(2)}) collective-permute-start(bf16[64,2048]{1,0:T(8,128)(2,1)S(1)} %collective-permute-done.2), channel_id=1, source_target_pairs={{0,64},{64,128},{128,192},{192,256},{256,320},{320,384},{384,448},... | collective-permute-start | bytes 786440 | tf_op jit(solution)/shard_map/ppermute | solution.py:24
  54.5 6.2 %copy-start.1 = (bf16[512,2048]{1,0:T(8,128)(2,1)}, bf16[512,2048]{1,0:T(8,128)(2,1)S(1)}, u32[]{:S(2)}) copy-start(bf16[512,2048]{1,0:T(8,128)(2,1)S(1)} %constant_dynamic-update-slice_fusion.own_ref) | copy-start | bytes 6291460
  54.5 6.2 %collective-permute-start.7 = (bf16[512,2048]{1,0:T(8,128)(2,1)S(1)}, bf16[512,2048]{1,0:T(8,128)(2,1)}, u32[]{:S(2)}, u32[]{:S(2)}) collective-permute-start(bf16[512,2048]{1,0:T(8,128)(2,1)S(1)} %constant_dynamic-update-slice_fusion.own_ref), channel_id=1, source_target_pairs={{0,32},{32,0},{1,33},{33,1},{2,34},{34,2},{3,35},{35,3},{4,36},{36... | collective-permute-start | bytes 6291464 | tf_op jit(solution)/shard_map/ppermute | solution.py:14
  60.7 15.9 %copy-start.7 = (s32[6144]{0:T(1024)S(1)}, s32[6144]{0:T(1024)}, u32[]{:S(2)}) copy-start(s32[6144]{0:T(1024)} %param.19) | copy-start | bytes 73732
  66.7 33.3 %copy-start.6 = (bf16[384,32]{0,1:T(8,128)(2,1)S(1)}, bf16[384,32]{0,1:T(8,128)(2,1)}, u32[]{:S(2)}) copy-start(bf16[384,32]{0,1:T(8,128)(2,1)} %param.11) | copy-start | bytes 73732
  66.7 33.2 %all-to-all-start.1 = ((bf16[32,32,384]{2,1,0:T(8,128)(2,1)}), bf16[32,32,384]{2,1,0:T(8,128)(2,1)S(1)}, u32[]{:S(2)}, u32[]{:S(2)}) async-start(bf16[32,32,384]{2,1,0:T(8,128)(2,1)} %bitcast.21), calls=%async_computation.1 | async-start | bytes 1572864 | tf_op jit(solution)/shard_map/all_to_all | solution.py:240
  138.0 11.0 %copy-start.2 = (bf16[8,32,1152]{2,1,0:T(8,128)(2,1)}, bf16[8,32,1152]{2,1,0:T(8,128)(2,1)S(1)}, u32[]{:S(2)}) copy-start(bf16[8,32,1152]{2,1,0:T(8,128)(2,1)S(1)} %all_to_all.26) | copy-start | bytes 1769476
  138.0 18.0 %collective-permute-start.8 = (bf16[256,1152]{1,0:T(8,128)(2,1)S(1)}, bf16[256,1152]{1,0:T(8,128)(2,1)S(1)}, u32[]{:S(2)}, u32[]{:S(2)}) collective-permute-start(bf16[256,1152]{1,0:T(8,128)(2,1)S(1)} %bitcast.22), channel_id=1, source_target_pairs={{0,8},{8,16},{16,24},{24,0},{1,9},{9,17},{17,25},{25,1},{2,10},{10... | collective-permute-start | bytes 1769480 | tf_op jit(solution)/shard_map/ppermute | solution.py:24
  140.5 17.4 %collective-permute-start.9 = (bf16[256,1152]{1,0:T(8,128)(2,1)S(1)}, bf16[256,1152]{1,0:T(8,128)(2,1)}, u32[]{:S(2)}, u32[]{:S(2)}) collective-permute-start(bf16[256,1152]{1,0:T(8,128)(2,1)S(1)} %bitcast.23), channel_id=1, source_target_pairs={{0,24},{8,0},{16,8},{24,16},{1,25},{9,1},{17,9},{25,17},{2,26},{10... | collective-permute-start | bytes 1769480 | tf_op jit(solution)/shard_map/ppermute | solution.py:24
  146.0 3.0 %copy-start.9 = (bf16[1024]{0:T(1024)(128)(2,1)S(1)}, bf16[1024]{0:T(1024)(128)(2,1)}, u32[]{:S(2)}) copy-start(bf16[1024]{0:T(1024)(128)(2,1)} %param.15) | copy-start | bytes 6148
  146.0 3.1 %copy-start.12 = (s32[4]{0:T(128)S(1)}, s32[4]{0:T(128)}, u32[]{:S(2)}) copy-start(s32[4]{0:T(128)} %constant.72.clone) | copy-start | bytes 52
  156.0 10.0 %copy-start.3 = (bf16[256,1152]{1,0:T(8,128)(2,1)}, bf16[256,1152]{1,0:T(8,128)(2,1)S(1)}, u32[]{:S(2)}) copy-start(bf16[256,1152]{1,0:T(8,128)(2,1)S(1)} %collective-permute-done.8.behind_ref) | copy-start | bytes 1769476
  156.0 10.8 %collective-permute-start.10 = (bf16[128,1152]{1,0:T(8,128)(2,1)S(1)}, bf16[128,1152]{1,0:T(8,128)(2,1)S(1)}, u32[]{:S(2)}, u32[]{:S(2)}) collective-permute-start(bf16[128,1152]{1,0:T(8,128)(2,1)S(1)} %slice.8), channel_id=1, source_target_pairs={{0,8},{8,16},{16,24},{24,0},{1,9},{9,17},{17,25},{25,1},{2,10},{10... | collective-permute-start | bytes 884744 | tf_op jit(solution)/shard_map/ppermute | solution.py:24
  158.9 10.1 %collective-permute-start.11 = (bf16[128,1152]{1,0:T(8,128)(2,1)S(1)}, bf16[128,1152]{1,0:T(8,128)(2,1)S(1)}, u32[]{:S(2)}, u32[]{:S(2)}) collective-permute-start(bf16[128,1152]{1,0:T(8,128)(2,1)S(1)} %slice.9), channel_id=1, source_target_pairs={{0,24},{8,0},{16,8},{24,16},{1,25},{9,1},{17,9},{25,17},{2,26},{10... | collective-permute-start | bytes 884744 | tf_op jit(solution)/shard_map/ppermute | solution.py:24
  166.8 0.7 copy-start.10
  169.0 0.7 copy-start.11
